TPU v7x, 32 devices: a whole 2x2x4 slice. The times are simulated.
32 devices in a mesh: rep: 8 (over z, x), fsdp: 4 (over y, core).
Axes of the slice: x: 2, y: 2, z: 4, core: 2. Of those that a mesh axis runs over, the one named last changes fastest.
Arguments:
- activations: bfloat16 [8, 512, 8192], P('rep', 'fsdp'), may hold values from -6 to 6
- cotangent: bfloat16 [8, 512, 1024], P('rep', 'fsdp'), may hold values from -0.02734375 to 0.02734375
- momentum: float32 [8, 8192, 1024], P('rep', 'fsdp'), may hold values from -6 to 6
- positions: int32 [8, 2048, 32], P('rep', 'fsdp'), may hold values from 0 to 4095, as said below
Outputs:
- new_momentum: float32 [8, 8192, 1024], P('rep', 'fsdp')
- step: float32 [8192, 1024], P('fsdp')
Inputs may be any that keep to these rules, and one draw needn't show every extreme that they name: Within one replica and one group the 32 positions are distinct.
All inputs are finite; a program needn't handle non-finite values.
Results may differ from a plain program's by a relative error of at most 0.0017.
Values may be sent and summed in bfloat16 or wider, within the bound.
No kernel may reach another device: no remote copies, remote signals or barrier semaphores. Data moves between devices by JAX's collectives and lax.ppermute only.
A program may use at most 192 MiB of HBM per device.

v0:
```python
import jax
import jax.numpy as jnp
from jax import lax
from jax.sharding import PartitionSpec as P

GROUP = 64


momentum_decay = 0.999
sharpness = 4.0


def dct_table(extent):
    frequency = jnp.arange(extent, dtype=jnp.float32)[:, None]
    location = jnp.arange(extent, dtype=jnp.float32)[None, :]
    cosines = jnp.cos(jnp.pi * (2.0 * location + 1.0) * frequency / (2.0 * extent)) * jnp.sqrt(
        2.0 / extent
    )
    return jnp.where(frequency == 0.0, cosines * jnp.sqrt(0.5), cosines)


def forward_dct(spatial, cosines):
    row_count, col_count = spatial.shape
    extent = cosines.shape[0]
    blocks = spatial.reshape(row_count // extent, extent, col_count // extent, extent)
    coeffs = jnp.einsum(
        "hi,piqj,lj->hlpq", cosines, blocks, cosines, precision=lax.Precision.HIGHEST
    )
    return coeffs.reshape(extent, extent, -1)


def inverse_dct(coeffs, cosines, row_count, col_count):
    extent = cosines.shape[0]
    grid_form = coeffs.reshape(extent, extent, row_count // extent, col_count // extent)
    spatial = jnp.einsum(
        "hi,hlpq,lj->piqj", cosines, grid_form, cosines, precision=lax.Precision.HIGHEST
    )
    return spatial.reshape(row_count, col_count)


def one_hots(spot_list, extent):
    levels = jnp.arange(extent, dtype=jnp.int32)[:, None]
    expanded = spot_list[..., None, :]
    upper_hot = (expanded // extent == levels).astype(jnp.float32)
    lower_hot = (expanded % extent == levels).astype(jnp.float32)
    return (upper_hot, lower_hot)


def per_device(activations, cotangent, momentum, positions):
    tokens = activations[0]
    upstream = cotangent[0]
    moment = momentum[0]
    row_count, col_count = moment.shape
    tok_rows = tokens.shape[0]
    cosines = dct_table(GROUP)
    columns = lax.all_to_all(tokens, "fsdp", split_axis=1, concat_axis=0, tiled=True)
    incoming = lax.all_gather(upstream, "fsdp", axis=0, tiled=True)

    def add_source(source, partial_sum):
        left_block = lax.dynamic_slice_in_dim(columns, source * tok_rows, tok_rows, 0)
        right_block = lax.dynamic_slice_in_dim(incoming, source * tok_rows, tok_rows, 0)
        product = lax.dot_general(
            left_block, right_block, (((0,), (0,)), ((), ())), preferred_element_type=jnp.float32
        )
        rounded = lax.optimization_barrier(product.astype(jnp.bfloat16))
        return partial_sum + rounded.astype(jnp.float32)

    gradient = lax.fori_loop(
        0, incoming.shape[0] // tok_rows, add_source, jnp.zeros((row_count, col_count), jnp.float32)
    )
    updated = momentum_decay * moment + gradient
    coeffs = forward_dct(updated, cosines)
    spot_list = positions[0].T
    upper_hot, lower_hot = one_hots(spot_list, GROUP)
    picked = jnp.einsum("hln,jhn->jln", coeffs, upper_hot, precision=lax.Precision.HIGHEST)
    values = jnp.sum(picked * lower_hot, axis=1)
    own_groups = jnp.einsum(
        "jhn,jln->hln", upper_hot * values[:, None, :], lower_hot, precision=lax.Precision.HIGHEST
    )
    next_moment = updated - inverse_dct(own_groups, cosines, row_count, col_count)
    part_values = lax.all_gather(values[None], "rep", axis=0, tiled=True)
    part_spots = lax.all_gather(spot_list[None], "rep", axis=0, tiled=True)
    upper_all, lower_all = one_hots(part_spots, GROUP)
    dense_sum = jnp.einsum(
        "kjhn,kjln->hln",
        upper_all * part_values[:, :, None, :],
        lower_all,
        precision=lax.Precision.HIGHEST,
    )
    update = inverse_dct(dense_sum, cosines, row_count, col_count)
    return (next_moment[None], jnp.tanh(sharpness * update))


def solution(mesh):
    return jax.shard_map(
        per_device,
        mesh=mesh,
        in_specs=(
            P("rep", "fsdp", None),
            P("rep", "fsdp", None),
            P("rep", "fsdp", None),
            P("rep", "fsdp", None),
        ),
        out_specs=(P("rep", "fsdp", None), P("fsdp", None)),
        check_vma=False,
    )
```

profile of v0, /device:TPU:0, one launch (start us, length us, event | category | flops | bytes accessed | tf_op | source)
XLA Modules:
  0.0 610.3 jit_solution(2100032833197797229)
XLA Ops:
  18.3 32.8 %all-gather.1 = s32[256,512]{1,0:T(8,128)S(1)} all-gather(s32[32,512]{1,0:T(8,128)S(1)} %bitcast.68), channel_id=3, replica_groups=mesh['rep'=8,'fsdp'=4] {'rep'}, dimensions={0}, use_global_device_ids=true | all-gather | bytes 589824 | tf_op jit(solution)/shard_map/all_gather | solution.py:82
  57.4 41.6 %while.14 = (s32[]{:T(128)}, f32[2048,1024]{1,0:T(8,128)}, bf16[512,2048]{1,0:T(8,128)(2,1)S(1)}, bf16[512,1024]{1,0:T(8,128)(2,1)}, s32[]{:T(128)}, /*index=5*/s32[]{:T(128)}, s32[]{:T(128)}, s32[]{:T(128)}) while((s32[]{:T(128)}, f32[2048,1024]{1,0:T(8,128)}, bf16[512,2048]{1,0:T(8,128)(2,1)S(1)}, bf16[512,1024]{1,0:T(8,128)(2,1)}, ...), condition=%wide.region_1.2_spmd.clone, body=%wide.region_0.1_spmd.clone.sunk | while | flops 545259520 | bytes 25953428 | solution.py:68
  59.6 5.6 select_add_fusion.2
  67.5 9.0 %select_add_fusion.2 = f32[2048,1024]{1,0:T(8,128)} fusion(f32[2048,1024]{1,0:T(8,128)} %get-tuple-element.143, bf16[2048,1024]{1,0:T(8,128)(2,1)S(1)} %convolution_convert_fusion.2, pred[]{:T(512)S(6)} %compare.13), kind=kLoop, calls=%fused_computation.clone.1 | loop fusion | flops 6291456 | bytes 20971520 | tf_op jit(solution)/shard_map/while/body/eval_jaxpr/add | solution.py:66
  78.7 9.0 %select_add_fusion.2 = f32[2048,1024]{1,0:T(8,128)} fusion(f32[2048,1024]{1,0:T(8,128)} %get-tuple-element.143, bf16[2048,1024]{1,0:T(8,128)(2,1)S(1)} %convolution_convert_fusion.2, pred[]{:T(512)S(6)} %compare.13), kind=kLoop, calls=%fused_computation.clone.1 | loop fusion | flops 6291456 | bytes 20971520 | tf_op jit(solution)/shard_map/while/body/eval_jaxpr/add | solution.py:66
  89.9 9.0 %select_add_fusion.2 = f32[2048,1024]{1,0:T(8,128)} fusion(f32[2048,1024]{1,0:T(8,128)} %get-tuple-element.143, bf16[2048,1024]{1,0:T(8,128)(2,1)S(1)} %convolution_convert_fusion.2, pred[]{:T(512)S(6)} %compare.13), kind=kLoop, calls=%fused_computation.clone.1 | loop fusion | flops 6291456 | bytes 20971520 | tf_op jit(solution)/shard_map/while/body/eval_jaxpr/add | solution.py:66
  98.9 12.2 %bitcast_add_fusion = f32[2048,1024]{1,0:T(8,128)} fusion(f32[2048,1024]{1,0:T(8,128)} %get-tuple-element.81, f32[1,2048,1024]{2,1,0:T(8,128)} %param.8), kind=kLoop, calls=%fused_computation.19 | loop fusion | flops 4194304 | bytes 25165824 | tf_op jit(solution)/shard_map/add | solution.py:71
  111.2 13.3 %reshape.97 = f32[32,64,16,64]{3,2,1,0:T(8,128)} reshape(f32[2048,1024]{1,0:T(8,128)} %bitcast_add_fusion) | data formatting | bytes 16777216 | tf_op jit(solution)/shard_map/reshape | solution.py:25
  124.5 29.2 %fusion.9 = f32[32,16,64,64]{2,3,1,0:T(8,128)} fusion(f32[32,64,16,64]{3,2,1,0:T(8,128)} %reshape.97, f32[64]{0:T(128)S(1)} %add_multiply_fusion, pred[64]{0:T(512)(128)(4,1)S(1)} %iota_compare_fusion.11), kind=kOutput, calls=%fused_computation.13 | convolution fusion | flops 1610633216 | bytes 16777536 | tf_op jit(solution)/shard_map/hi,piqj,lj->hlpq/dot_general | solution.py:26
  153.7 23.7 %fusion.30 = f32[32,16,64,64]{3,2,1,0:T(8,128)S(1)} fusion(f32[32,16,64,64]{2,3,1,0:T(8,128)} %fusion.9, f32[64]{0:T(128)S(1)} %add_multiply_fusion, pred[64]{0:T(512)(128)(4,1)S(1)} %iota_compare_fusion.11), kind=kOutput, calls=%fused_computation.53 | convolution fusion | flops 1610633216 | bytes 16777536 | tf_op jit(solution)/shard_map/hi,piqj,lj->hlpq/dot_general | solution.py:26
  177.4 12.4 %fusion.11 = f32[32,512]{0,1:T(8,128)S(1)} fusion(s32[32,512]{0,1:T(8,128)S(1)} %copy.34, f32[64,64,512]{1,0,2:T(8,128)S(1)} %bitcast.61, s32[32,512]{0,1:T(8,128)S(1)} %copy.35), kind=kOutput, calls=%fused_computation.18 | convolution fusion | flops 809484288 | bytes 8585216 | tf_op jit(solution)/shard_map/hln,jhn->jln/dot_general | solution.py:75
  189.9 28.4 %fusion.12 = f32[512,64,64]{2,1,0:T(8,128)} fusion(f32[32,512]{0,1:T(8,128)S(1)} %fusion.11, s32[32,512]{0,1:T(8,128)S(1)} %copy.35, s32[32,512]{0,1:T(8,128)S(1)} %copy.34), kind=kOutput, calls=%fused_computation.21 | convolution fusion | flops 808452096 | bytes 8585216 | tf_op jit(solution)/shard_map/jhn,jln->hln/dot_general | solution.py:77
  218.3 31.2 %all-gather.2 = f32[256,512]{1,0:T(8,128)S(1)} all-gather(f32[32,512]{1,0:T(8,128)S(1)} %copy.42), channel_id=4, replica_groups=mesh['rep'=8,'fsdp'=4] {'rep'}, dimensions={0}, use_global_device_ids=true | all-gather | bytes 589824 | tf_op jit(solution)/shard_map/all_gather | solution.py:81
  250.2 55.5 %fusion.28 = f32[64,32,16,64]{0,3,2,1:T(8,128)} fusion(f32[64,64,32,16]{0,1,3,2:T(8,128)} %bitcast.62, f32[64]{0:T(128)S(1)} %add_multiply_fusion, pred[64]{0:T(512)(128)(4,1)S(1)} %iota_compare_fusion.11), kind=kOutput, calls=%fused_computation.51 | convolution fusion | flops 1610633216 | bytes 16777536 | tf_op jit(solution)/shard_map/hi,hlpq,lj->piqj/dot_general | solution.py:35
  305.7 23.2 %convolution_bitcast_fusion = f32[32,64,16,64]{3,1,2,0:T(8,128)S(1)} fusion(f32[64,32,16,64]{0,3,2,1:T(8,128)} %fusion.28, f32[64]{0:T(128)S(1)} %add_multiply_fusion, pred[64]{0:T(512)(128)(4,1)S(1)} %iota_compare_fusion.11), kind=kOutput, calls=%fused_computation.16 | convolution fusion | flops 1610633216 | bytes 16777536 | tf_op jit(solution)/shard_map/hi,hlpq,lj->piqj/dot_general | solution.py:35
  329.0 13.7 %copy.39 = f32[32,64,16,64]{3,2,1,0:T(8,128)} copy(f32[32,64,16,64]{3,1,2,0:T(8,128)S(1)} %convolution_bitcast_fusion) | data formatting | bytes 16777216 | tf_op jit(solution)/shard_map/hi,hlpq,lj->piqj/transpose | solution.py:35
  342.7 14.5 %reshape.100 = f32[2048,1024]{1,0:T(8,128)} reshape(f32[32,64,16,64]{3,2,1,0:T(8,128)} %copy.39) | data formatting | bytes 16777216 | tf_op jit(solution)/shard_map/reshape | solution.py:38
  357.2 12.3 %subtract_bitcast_fusion = f32[1,2048,1024]{2,1,0:T(8,128)} fusion(f32[2048,1024]{1,0:T(8,128)} %bitcast_add_fusion, f32[2048,1024]{1,0:T(8,128)} %reshape.100), kind=kLoop, calls=%fused_computation.20 | loop fusion | flops 2097152 | bytes 25165824 | tf_op jit(solution)/shard_map/broadcast_in_dim | solution.py:91
  369.5 40.7 %fusion.92 = f32[8,32,64,512]{2,1,0,3:T(8,128)} fusion(f32[8,32,512]{1,0,2:T(8,128)S(1)} %copy.43, s32[8,32,512]{1,0,2:T(8,128)S(1)} %copy-done.1), kind=kLoop, calls=%fused_computation.6.clone.2 | loop fusion | flops 16777216 | bytes 34603008 | tf_op jit(solution)/shard_map/kjhn,kjln->hln/dot_general | solution.py:84
  410.2 85.3 %fusion.3 = f32[512,64,64,1]{2,1,3,0:T(8,128)} fusion(s32[8,32,512]{1,0,2:T(8,128)S(1)} %copy-done, f32[8,32,64,512]{2,1,0,3:T(8,128)} %fusion.92), kind=kOutput, calls=%fused_computation.5 | convolution fusion | flops 6450839552 | bytes 42467328 | tf_op jit(solution)/shard_map/kjhn,kjln->hln/dot_general | solution.py:84
  495.5 55.2 %fusion.25 = f32[64,32,16,64]{0,3,2,1:T(8,128)} fusion(f32[64,64,32,16]{0,1,3,2:T(8,128)} %bitcast.63, f32[64]{0:T(128)S(1)} %add_multiply_fusion, pred[64]{0:T(512)(128)(4,1)S(1)} %iota_compare_fusion.11), kind=kOutput, calls=%fused_computation.48 | convolution fusion | flops 1610633216 | bytes 16777536 | tf_op jit(solution)/shard_map/hi,hlpq,lj->piqj/dot_general | solution.py:35
  550.7 24.3 %tanh_bitcast_fusion = f32[32,64,16,64]{3,1,2,0:T(8,128)S(1)} fusion(f32[64,32,16,64]{0,3,2,1:T(8,128)} %fusion.25, f32[64]{0:T(128)S(1)} %add_multiply_fusion, pred[64]{0:T(512)(128)(4,1)S(1)} %iota_compare_fusion.11), kind=kOutput, calls=%fused_computation.15 | convolution fusion | flops 1612730368 | bytes 16777536 | tf_op jit(solution)/shard_map/hi,hlpq,lj->piqj/dot_general | solution.py:35
  575.0 13.7 %copy.45 = f32[32,64,16,64]{3,2,1,0:T(8,128)} copy(f32[32,64,16,64]{3,1,2,0:T(8,128)S(1)} %tanh_bitcast_fusion) | data formatting | bytes 16777216 | tf_op jit(solution)/shard_map/tanh | solution.py:91
  588.8 14.5 %tanh.11 = f32[2048,1024]{1,0:T(8,128)} reshape(f32[32,64,16,64]{3,2,1,0:T(8,128)} %copy.45) | data formatting | bytes 16777216 | tf_op jit(solution)/shard_map/tanh | solution.py:91
  (28 shorter events, 27.1 us)
Async XLA Ops:
  7.2 10.8 %copy-start.2 = (s32[1,512,32]{1,2,0:T(8,128)S(1)}, s32[1,512,32]{1,2,0:T(8,128)}, u32[]{:S(2)}) copy-start(s32[1,512,32]{1,2,0:T(8,128)} %param.9) | copy-start | bytes 196612
  7.2 50.2 %all-gather.5.cloned.1.call-start = ((), (), s32[]{:S(2)}) async-start(), calls=%async_computation.1 | async-start | bytes 1310720 | tf_op jit(solution)/shard_map/all_gather | solution.py:57
  13.7 43.6 %all-to-all-start = ((bf16[128,4,2048]{2,0,1:T(8,128)(2,1)}), bf16[128,4,2048]{2,0,1:T(8,128)(2,1)S(1)}, u32[]{:S(2)}, u32[]{:S(2)}) async-start(bf16[128,4,2048]{2,0,1:T(8,128)(2,1)} %copy.33), calls=%async_computation | async-start | bytes 4194304 | tf_op jit(solution)/shard_map/all_to_all | solution.py:56
  357.2 12.3 %copy-start.1 = (s32[8,32,512]{1,0,2:T(8,128)S(1)}, s32[8,32,512]{1,0,2:T(8,128)}, u32[]{:S(2)}) copy-start(s32[8,32,512]{1,0,2:T(8,128)} %copy.41) | copy-start | bytes 1572868
  369.5 40.7 %copy-start = (s32[8,32,512]{1,0,2:T(8,128)S(1)}, s32[8,32,512]{1,0,2:T(8,128)}, u32[]{:S(2)}) copy-start(s32[8,32,512]{1,0,2:T(8,128)} %copy.40) | copy-start | bytes 1572868
Sparse Core Ops, SparseCore 0:
  9.5 25.1 all-gather.4
where the time goes:
time: 618 us; the launch traced here: 610 us
  matrix products  346 us (56%)
  other arithmetic  99.2 us (16%)
  local copies, waits for them, and re-layouts  81.6 us (13%)
  blocking collectives  64 us (10%)
  between operations  14.4 us (2%)
    dot_general x4, matrix products, inverse_dct(): jnp.einsum('hi,hlpq,lj->piqj', cosines, grid_form, cosines, precision=lax...  158 us
    dot_general x1, matrix products, per_device(): jnp.einsum('kjhn,kjln->hln', upper_all * part_values[:, :, None, :], lowe...  85.3 us
    dot_general x2, matrix products, forward_dct(): jnp.einsum('hi,piqj,lj->hlpq', cosines, blocks, cosines, precision=lax.Pr...  52.9 us
    dot_general x1, other arithmetic, per_device(): jnp.einsum('kjhn,kjln->hln', upper_all * part_values[:, :, None, :], lowe...  40.7 us
    all_gather x1, blocking collectives, per_device(): part_spots = lax.all_gather(spot_list[None], 'rep', axis=0, tiled=True)  32.8 us
    add x4, other arithmetic, add_source(): return partial_sum + rounded.astype(jnp.float32)  32.6 us
    all_gather x1, blocking collectives, per_device(): part_values = lax.all_gather(values[None], 'rep', axis=0, tiled=True)  31.2 us
    dot_general x1, matrix products, per_device(): jnp.einsum('jhn,jln->hln', upper_hot * values[:, None, :], lower_hot, pre...  28.4 us
  transfers between devices with their start and end apart: 2, of which 0 were waited for; matrix products, arithmetic and copies ran while one was open for 1% of the time, Pallas kernels for 0%

commit v1 on v0

v1 whole, which is shorter than its diff:
```python
import functools

import jax
import jax.numpy as jnp
import numpy as np
from jax import lax
from jax.experimental import pallas as pl
from jax.experimental.pallas import tpu as pltpu
from jax.sharding import PartitionSpec as P

GROUP = 64
LANES = 128
WIDE = 256
CHUNKS = 2


momentum_decay = 0.999
sharpness = 4.0


def dct_table(extent):
    frequency = np.arange(extent, dtype=np.float64)[:, None]
    location = np.arange(extent, dtype=np.float64)[None, :]
    cosines = np.cos(np.pi * (2.0 * location + 1.0) * frequency / (2.0 * extent))
    cosines = cosines * np.sqrt(2.0 / extent)
    cosines[0] *= np.sqrt(0.5)
    return cosines.astype(np.float32)


def bf16_parts(x):
    high = x.astype(jnp.bfloat16)
    return high, (x - high.astype(np.float32)).astype(jnp.bfloat16)


def forward_matrix(cosines):
    high, low = bf16_parts(np.kron(np.eye(WIDE // GROUP, dtype=np.float32), cosines.T))
    return np.concatenate([high, high, low], axis=0)


def side_matrix(cosines):
    high, low = bf16_parts(cosines.T)
    return np.concatenate([high, high, low, low], axis=1)


def right_matrix(cosines):
    high, low = bf16_parts(np.kron(np.eye(LANES // GROUP, dtype=np.float32), cosines))
    upper = np.concatenate([high, low], axis=1)
    return np.concatenate([upper, np.concatenate([high, np.zeros_like(low)], axis=1)], axis=0)


def all_matrices(cosines):
    parts = [forward_matrix(cosines), right_matrix(cosines), side_matrix(cosines)]
    return np.concatenate(parts, axis=0)


FORWARD = slice(0, 3 * WIDE)
RIGHT = slice(3 * WIDE, 4 * WIDE)
SIDE = slice(4 * WIDE, 4 * WIDE + GROUP)


def halves(x):
    high = x.astype(jnp.bfloat16)
    return high, (x - high.astype(jnp.float32)).astype(jnp.bfloat16)


def nt_dot(a, b):
    return lax.dot_general(a, b, (((1,), (1,)), ((), ())), preferred_element_type=jnp.float32)


def right_product(x, stacked):
    high, low = halves(x)
    return jnp.dot(
        jnp.concatenate([high, low, high], axis=1), stacked, preferred_element_type=jnp.float32
    )


def local_kernel(sources, kept, *refs):
    token_refs, upstream_refs = refs[:sources], refs[sources : 2 * sources]
    moment_ref, spot_ref, matrix_ref = refs[2 * sources : 2 * sources + 3]
    next_ref, value_ref, half_ref = refs[-3:]
    rows, cols = moment_ref.shape
    per_row = LANES // kept
    lane = lax.broadcasted_iota(jnp.int32, (8, LANES), 1)
    first = lane < 2 * kept
    shift = GROUP * ((lane // kept) % 2)
    side = matrix_ref[SIDE, :].astype(jnp.float32)
    side = side[:, :LANES] + side[:, LANES:]
    table = [side[8 * k : 8 * k + 8, :] for k in range(GROUP // 8)]
    lane_group = lax.broadcasted_iota(jnp.int32, (WIDE, LANES), 1) // kept
    row_group = lax.broadcasted_iota(jnp.int32, (WIDE, LANES), 0) // GROUP
    diagonal = lane_group == row_group
    zero = jnp.zeros((), jnp.bfloat16)
    gradient = lax.dot_general(
        jnp.concatenate([r[...] for r in token_refs], axis=0),
        jnp.concatenate([r[...] for r in upstream_refs], axis=0),
        (((0,), (0,)), ((), ())),
        preferred_element_type=jnp.float32,
    )
    next_ref[...] = momentum_decay * moment_ref[...] + gradient
    for c in range(cols // WIDE):
        span = slice(c * WIDE, c * WIDE + WIDE)
        half_ref[:, span] = right_product(next_ref[:, span], matrix_ref[FORWARD, :])
    for p in range(rows // GROUP):
        for c in range(cols // WIDE):
            at = p * (cols // WIDE) + c
            spots = jnp.broadcast_to(spot_ref[0, at : at + 1, :], (8, LANES))
            upper, lower = spots // GROUP, spots % GROUP
            where = lower + shift
            total = jnp.zeros((8, LANES), jnp.float32)
            upper_rows, lower_rows = [], []
            for k in range(GROUP // 8):
                block = slice(p * GROUP + 8 * k, p * GROUP + 8 * k + 8)
                low_half = half_ref[block, c * WIDE : c * WIDE + LANES]
                high_half = half_ref[block, c * WIDE + LANES : c * WIDE + WIDE]
                one = jnp.take_along_axis(low_half, where, axis=1)
                two = jnp.take_along_axis(high_half, where, axis=1)
                up = jnp.take_along_axis(table[k], upper, axis=1)
                total = total + jnp.where(first, one, two) * up
                upper_rows.append(up)
                lower_rows.append(jnp.take_along_axis(table[k], lower, axis=1))
            value = jnp.sum(total, axis=0, keepdims=True)
            value_ref[0, at : at + 1, :] = value
            s_high, s_low = halves(jnp.concatenate(upper_rows, axis=0) * value)
            b_high, b_low = halves(jnp.concatenate(lower_rows, axis=0))
            r_high = jnp.where(diagonal, jnp.concatenate([b_high] * per_row, axis=0), zero)
            r_low = jnp.where(diagonal, jnp.concatenate([b_low] * per_row, axis=0), zero)
            own = nt_dot(
                jnp.concatenate([s_high, s_low, s_high], axis=1),
                jnp.concatenate([r_high, r_high, r_low], axis=1),
            )
            block, span = slice(p * GROUP, p * GROUP + GROUP), slice(c * WIDE, c * WIDE + WIDE)
            next_ref[block, span] = next_ref[block, span] - own


def shared_kernel(kept, replicas, *refs):
    value_refs, spot_refs = refs[:replicas], refs[replicas : 2 * replicas]
    matrix_ref = refs[2 * replicas]
    step_ref, dense_ref = refs[-2:]
    values = [r[0] for r in value_refs]
    spots = [r[0] for r in spot_refs]
    depth = len(values) * kept
    rows, cols = step_ref.shape
    per_row = LANES // kept
    level = lax.broadcasted_iota(jnp.int32, (GROUP, depth), 0)
    level = level.astype(jnp.float32).astype(jnp.bfloat16)
    zero = jnp.zeros((), jnp.bfloat16)
    one = jnp.ones((), jnp.bfloat16)

    def filled(x, at):
        tile = jnp.broadcast_to(x[at : at + 1], (16, depth)).astype(jnp.bfloat16)
        return jnp.concatenate([tile] * (GROUP // 16), axis=0)

    for a in range(per_row):
        span = slice(a * kept, a * kept + kept)
        group_values = jnp.concatenate([v[:, span] for v in values], axis=1)
        group_spots = jnp.concatenate([s[:, span] for s in spots], axis=1)
        high, low = halves(group_values)
        high, low = high.astype(jnp.float32), low.astype(jnp.float32)
        upper = (group_spots // GROUP).astype(jnp.float32)
        lower = (group_spots % GROUP).astype(jnp.float32)
        for at in range(group_values.shape[0]):
            p, c = at // (cols // WIDE), at % (cols // WIDE)
            hot_upper = jnp.where(level == filled(upper, at), one, zero)
            match = level == filled(lower, at)
            hot_high = jnp.where(match, filled(high, at), zero)
            hot_low = jnp.where(match, filled(low, at), zero)
            dense = nt_dot(hot_upper, hot_high) + nt_dot(hot_upper, hot_low)
            place = slice(c * WIDE + a * GROUP, c * WIDE + a * GROUP + GROUP)
            dense_ref[p * GROUP : p * GROUP + GROUP, place] = dense
    pieces = []
    for c in range(cols // WIDE):
        parts = []
        for p in range(rows // GROUP):
            tile = dense_ref[p * GROUP : p * GROUP + GROUP, c * WIDE : c * WIDE + WIDE]
            high, low = halves(tile)
            stack = jnp.concatenate([high, low, high], axis=0)
            parts.append(jnp.dot(matrix_ref[SIDE, : 3 * GROUP], stack, preferred_element_type=jnp.float32))
        high, low = halves(jnp.concatenate(parts, axis=0))
        for b in range(WIDE // LANES):
            span = slice(b * LANES, b * LANES + LANES)
            pieces.append(jnp.concatenate([high[:, span], low[:, span]], axis=1))
    product = jnp.dot(
        jnp.concatenate(pieces, axis=0), matrix_ref[RIGHT, :], preferred_element_type=jnp.float32
    )
    for b in range(len(pieces)):
        part = product[b * rows : b * rows + rows]
        update = part[:, :LANES] + part[:, LANES:]
        step_ref[:, b * LANES : b * LANES + LANES] = jnp.tanh(sharpness * update)


def swap(x, axis, count, offset):
    return lax.ppermute(x, axis, [(i, i ^ offset) for i in range(count)])


def spread(x, count):
    even = [x]
    even += [swap(x, "rep", count, offset) for offset in range(2, count, 2)]
    odd = [swap(part, "rep", count, 1) for part in even]
    return even + odd


def local_call(sources, kept, blocks, at, columns, incoming, moment, spots, consts, previous):
    row_count, col_count = moment.shape
    tok = columns[0].shape[0]
    spot_rows = spots.shape[1]
    whole = pl.BlockSpec(memory_space=pltpu.VMEM)
    aliased = [] if previous is None else [previous]
    rows = blocks * WIDE
    return pl.pallas_call(
        functools.partial(local_kernel, sources, kept),
        grid=(blocks,),
        in_specs=[pl.BlockSpec((tok, WIDE), lambda i: (0, i))] * sources
        + [whole] * sources
        + [
            pl.BlockSpec((WIDE, col_count), lambda i: (at + i, 0)),
            pl.BlockSpec((1, spot_rows, LANES), lambda i: (at + i, 0, 0)),
        ]
        + [whole] * len(consts)
        + [pl.BlockSpec(memory_space=pl.ANY)] * len(aliased),
        out_specs=[
            pl.BlockSpec((WIDE, col_count), lambda i: (at + i, 0)),
            pl.BlockSpec((1, spot_rows, LANES), lambda i: (i, 0, 0)),
        ],
        out_shape=[
            jax.ShapeDtypeStruct((row_count, col_count), jnp.float32),
            jax.ShapeDtypeStruct((blocks, spot_rows, LANES), jnp.float32),
        ],
        input_output_aliases={2 * sources + 2 + len(consts): 0} if aliased else {},
        scratch_shapes=[pltpu.VMEM((WIDE, col_count), jnp.float32)],
        compiler_params=pltpu.CompilerParams(vmem_limit_bytes=48 * 2**20),
        cost_estimate=pl.CostEstimate(
            flops=12 * rows * col_count * WIDE, bytes_accessed=8 * rows * col_count, transcendentals=0
        ),
        name="local",
    )(*columns, *incoming, moment, spots, *consts, *aliased)


def shared_call(kept, blocks, at, shape, values, spots, consts, previous):
    _, col_count = shape
    spot_rows = values[0].shape[1]
    whole = pl.BlockSpec(memory_space=pltpu.VMEM)
    replicas = len(values)
    aliased = [] if previous is None else [previous]
    rows = blocks * WIDE
    return pl.pallas_call(
        functools.partial(shared_kernel, kept, replicas),
        grid=(blocks,),
        in_specs=[pl.BlockSpec((1, spot_rows, LANES), lambda i: (i, 0, 0))] * replicas
        + [pl.BlockSpec((1, spot_rows, LANES), lambda i: (at + i, 0, 0))] * replicas
        + [whole] * len(consts)
        + [pl.BlockSpec(memory_space=pl.ANY)] * len(aliased),
        out_specs=pl.BlockSpec((WIDE, col_count), lambda i: (at + i, 0)),
        out_shape=jax.ShapeDtypeStruct(shape, jnp.float32),
        input_output_aliases={2 * replicas + len(consts): 0} if aliased else {},
        scratch_shapes=[pltpu.VMEM((WIDE, col_count), jnp.float32)],
        compiler_params=pltpu.CompilerParams(vmem_limit_bytes=48 * 2**20),
        cost_estimate=pl.CostEstimate(
            flops=12 * rows * col_count * WIDE, bytes_accessed=4 * rows * col_count, transcendentals=0
        ),
        name="shared",
    )(*values, *spots, *consts, *aliased)


def per_device(n_fsdp, n_rep, activations, cotangent, momentum, positions):
    tokens, upstream, moment = activations[0], cotangent[0], momentum[0]
    row_count, col_count = moment.shape
    kept = positions.shape[2]
    steps = row_count // WIDE
    chunks = min(CHUNKS, steps)
    blocks = steps // chunks
    spot_rows = WIDE * col_count // (GROUP * GROUP) * kept // LANES
    me = lax.axis_index("fsdp")
    half = n_fsdp // 2

    def pieces_of(k, me):
        return [
            lax.dynamic_slice_in_dim(
                tokens, (me ^ offset) * row_count + k * blocks * WIDE, blocks * WIDE, 1
            )
            for offset in range(n_fsdp)
        ]

    def exchange(pieces):
        out = [pieces[0]]
        for offset in range(1, n_fsdp):
            out.append(swap(pieces[offset], "fsdp", n_fsdp, offset))
        return out

    incoming = {0: upstream}
    offset = half
    while offset:
        for known in list(incoming):
            incoming[known ^ offset] = swap(incoming[known], "fsdp", n_fsdp, offset)
        offset //= 2
    pieces = pieces_of(0, me)
    me, positions, pieces = lax.optimization_barrier((me, positions, pieces))
    all_columns = [exchange(pieces)]
    for k in range(1, chunks):
        pieces = pieces_of(k, me)
        all_columns.append(exchange(pieces))
    spots = positions[0].reshape(steps, spot_rows, LANES)

    def settled(x):
        return jnp.where(me >= 0, x, jnp.zeros((), x.dtype))

    incoming = [settled(upstream)] + [incoming[i] for i in range(1, n_fsdp)]
    all_spots = spread(spots, n_rep)

    cosines = dct_table(GROUP)
    matrices = (settled(all_matrices(cosines)),)

    next_moment, step, gathered = None, None, []
    for k in range(chunks):
        next_moment, values = local_call(
            n_fsdp, kept, blocks, k * blocks, all_columns[k], incoming, moment, spots,
            matrices, next_moment,
        )
        gathered.append(spread(values, n_rep))
    for k in range(chunks):
        step = shared_call(
            kept, blocks, k * blocks, moment.shape, gathered[k], all_spots, matrices, step
        )
    return (next_moment[None], step)


def solution(mesh):
    spec = P("rep", "fsdp", None)
    return jax.shard_map(
        functools.partial(per_device, mesh.shape["fsdp"], mesh.shape["rep"]),
        mesh=mesh,
        in_specs=(spec, spec, spec, spec),
        out_specs=(spec, P("fsdp", None)),
        check_vma=False,
    )
```

time: 618 us -> 87.2 us (0.14); the launches traced: 610 us -> 86.9 us
  matrix products: 346 us -> 0 us
  other arithmetic: 99.2 us -> 2.07 us
  local copies, waits for them, and re-layouts: 81.6 us -> 3.6 us
  blocking collectives: 64 us -> 0 us
  Pallas kernels: 0 us -> 41.2 us
  starting transfers between devices: 4.3 us -> 34.6 us
  between operations: 14.4 us -> 0.73 us
    dot_general x13 -> x0, matrix products: 346 us -> none  [the longest x4 158 us: inverse_dct(): jnp.einsum('hi,hlpq,lj->piqj', cosines, grid_form, cosines, precision=lax...]
    all_gather x2 -> x0, blocking collectives: 64 us -> none  [the longest x1 32.8 us: per_device(): part_spots = lax.all_gather(spot_list[None], 'rep', axis=0, tiled=True)]
    add x5 -> x0, other arithmetic: 44.9 us -> none  [the longest x4 32.6 us: add_source(): return partial_sum + rounded.astype(jnp.float32)]
    pallas_call x0 -> x4, Pallas kernels: none -> 41.2 us  [the longest x2 22.2 us: local_call(): pl.pallas_call(functools.partial(local_kernel, sources, kept), grid=(bloc...]
    dot_general x1 -> x0, other arithmetic: 40.7 us -> none  [per_device(): jnp.einsum('kjhn,kjln->hln', upper_all * part_values[:, :, None, :], lowe...]
    ppermute x0 -> x30, starting transfers between devices: none -> 34.6 us  [swap(): return lax.ppermute(x, axis, [(i, i ^ offset) for i in range(count)])]
    tanh x2 -> x0, local copies, waits for them, and re-layouts: 28.2 us -> none  [per_device(): return (next_moment[None], jnp.tanh(sharpness * update))]
    reshape x2 -> x0, local copies, waits for them, and re-layouts: 27.8 us -> none  [the longest x1 14.5 us: inverse_dct(): return spatial.reshape(row_count, col_count)]
  transfers between devices with their start and end apart: 2 -> 30, of which waited for: 0 -> 2; matrix products, arithmetic and copies ran while one was open for 1% -> 7% of each run, Pallas kernels for 0% -> 36%
where the time goes in v1:
time: 87.2 us; the launch traced here: 86.9 us
  Pallas kernels  41.2 us (47%)
  starting transfers between devices  34.6 us (40%)
  waiting for transfers between devices  4.68 us (5%)
  local copies, waits for them, and re-layouts  3.6 us (4%)
  other arithmetic  2.07 us (2%)
    ppermute x30, starting transfers between devices, swap(): return lax.ppermute(x, axis, [(i, i ^ offset) for i in range(count)])  34.6 us
    pallas_call x2, Pallas kernels, local_call(): pl.pallas_call(functools.partial(local_kernel, sources, kept), grid=(bloc...  22.2 us
    pallas_call x2, Pallas kernels, shared_call(): pl.pallas_call(functools.partial(shared_kernel, kept, replicas), grid=(bl...  19 us
    ppermute x30, waiting for transfers between devices, swap(): return lax.ppermute(x, axis, [(i, i ^ offset) for i in range(count)])  4.68 us
    dynamic_slice x2, local copies, waits for them, and re-layouts, pieces_of(): lax.dynamic_slice_in_dim(tokens, (me ^ offset) * row_count + k * blocks *...  2.52 us
    select_n x2, other arithmetic, settled(): return jnp.where(me >= 0, x, jnp.zeros((), x.dtype))  2.07 us
  transfers between devices with their start and end apart: 30, of which 2 were waited for; matrix products, arithmetic and copies ran while one was open for 7% of the time, Pallas kernels for 36%

profile of v1, /device:TPU:0, one launch (start us, length us, event | category | flops | bytes accessed | tf_op | source)
XLA Modules:
  0.0 86.9 jit_solution(5625954861171681739)
XLA Ops:
  1.2 2.6 %collective-permute-start.4 = (bf16[128,1024]{1,0:T(8,128)(2,1)}, bf16[128,1024]{1,0:T(8,128)(2,1)S(1)}, u32[]{:S(2)}, u32[]{:S(2)}) collective-permute-start(bf16[128,1024]{1,0:T(8,128)(2,1)} %bitcast.24), channel_id=1, source_target_pairs={{0,2},{1,3},{2,0},{3,1},{4,6},{5,7},{6,4},{7,5},{8,10},{9,11},{10,... | collective-permute-start | bytes 786440 | tf_op jit(solution)/shard_map/ppermute | solution.py:192
  3.8 1.3 %dynamic-slice_bitcast_fusion.4 = (bf16[128,1024]{1,0:T(8,128)(2,1)S(1)}, bf16[128,1024]{1,0:T(8,128)(2,1)S(1)}, bf16[128,1024]{1,0:T(8,128)(2,1)S(1)}, bf16[128,1024]{1,0:T(8,128)(2,1)S(1)}) fusion(bf16[1,128,8192]{2,1,0:T(8,128)(2,1)} %param.5, s32[]{:T(128)S(6)} %select_n.43, s32[]{:T(128)S(6)} %select_n.42, s32[]{:T(128)S(6)} %select_n.41, s32[]{:T(128)S(6)} %select_n.40), kind=kLoop, calls=%fused_computation.5 | loop fusion | bytes 2097168 | tf_op jit(solution)/shard_map/dynamic_slice | solution.py:277
  6.1 3.7 %collective-permute-start.18 = (s32[8,16,128]{2,1,0:T(8,128)S(1)}, s32[8,16,128]{2,1,0:T(8,128)S(1)}, u32[]{:S(2)}, u32[]{:S(2)}) collective-permute-start(s32[8,16,128]{2,1,0:T(8,128)S(1)} %reshape_squeeze.3.refs_9_.refs_8_), channel_id=1, source_target_pairs={{0,24},{4,28},{8,16},{12,20},{16,8},{20,12},{24,0},{28,4},{1,25},{... | collective-permute-start | bytes 196616 | tf_op jit(solution)/shard_map/ppermute | solution.py:192
  10.3 1.1 %broadcast_select_fusion.refs_10_.refs_16_ = bf16[1088,256]{1,0:T(8,128)(2,1)S(1)} fusion(bf16[1088,256]{1,0:T(8,128)(2,1)} %constant.35.clone, pred[]{:T(512)S(6)} %ge.4), kind=kLoop, calls=%fused_computation | loop fusion | flops 278528 | bytes 1114113 | tf_op jit(solution)/shard_map/jit(_where)/select_n | solution.py:304
  13.1 1.3 %dynamic-slice_bitcast_fusion = (bf16[128,1024]{1,0:T(8,128)(2,1)S(1)}, bf16[128,1024]{1,0:T(8,128)(2,1)S(1)}, bf16[128,1024]{1,0:T(8,128)(2,1)S(1)}, bf16[128,1024]{1,0:T(8,128)(2,1)S(1)}) fusion(bf16[1,128,8192]{2,1,0:T(8,128)(2,1)} %param.5, s32[]{:T(128)S(6)} %select_n.47, s32[]{:T(128)S(6)} %select_n.45, s32[]{:T(128)S(6)} %select_n.44, s32[]{:T(128)S(6)} %select_n.46), kind=kLoop, calls=%fused_computation.1 | loop fusion | bytes 2097168 | tf_op jit(solution)/shard_map/dynamic_slice | solution.py:277
  14.4 1.0 %broadcast_select_fusion.1.refs_4_ = bf16[128,1024]{1,0:T(8,128)(2,1)S(1)} fusion(pred[]{:T(512)S(6)} %ge.4, bf16[1,128,1024]{2,1,0:T(8,128)(2,1)} %param.6), kind=kLoop, calls=%fused_computation.9 | loop fusion | flops 131072 | bytes 524289 | tf_op jit(solution)/shard_map/jit(_where)/select_n | solution.py:304
  15.4 1.2 %collective-permute-start.17 = (s32[8,16,128]{2,1,0:T(8,128)S(1)}, s32[8,16,128]{2,1,0:T(8,128)S(1)}, u32[]{:S(2)}, u32[]{:S(2)}) collective-permute-start(s32[8,16,128]{2,1,0:T(8,128)S(1)} %reshape_squeeze.3.refs_9_.refs_8_), channel_id=1, source_target_pairs={{0,16},{4,20},{8,24},{12,28},{16,0},{20,4},{24,8},{28,12},{1,17},{... | collective-permute-start | bytes 196616 | tf_op jit(solution)/shard_map/ppermute | solution.py:192
  16.6 2.8 %collective-permute-start.16 = (s32[8,16,128]{2,1,0:T(8,128)S(1)}, s32[8,16,128]{2,1,0:T(8,128)S(1)}, u32[]{:S(2)}, u32[]{:S(2)}) collective-permute-start(s32[8,16,128]{2,1,0:T(8,128)S(1)} %reshape_squeeze.3.refs_9_.refs_8_), channel_id=1, source_target_pairs={{0,8},{4,12},{8,0},{12,4},{16,24},{20,28},{24,16},{28,20},{1,9},{5... | collective-permute-start | bytes 196616 | tf_op jit(solution)/shard_map/ppermute | solution.py:192
  19.9 3.7 %collective-permute-done.8.refs_3_ = bf16[128,1024]{1,0:T(8,128)(2,1)S(1)} collective-permute-done((bf16[128,1024]{1,0:T(8,128)(2,1)S(1)}, bf16[128,1024]{1,0:T(8,128)(2,1)S(1)}, u32[]{:S(2)}, u32[]{:S(2)}) %collective-permute-start.8) | collective-permute-done | bytes 262176 | tf_op jit(solution)/shard_map/ppermute | solution.py:192
  23.7 1.0 %collective-permute-start = (bf16[128,1024]{1,0:T(8,128)(2,1)S(1)}, bf16[128,1024]{1,0:T(8,128)(2,1)S(1)}, u32[]{:S(2)}, u32[]{:S(2)}) collective-permute-start(bf16[128,1024]{1,0:T(8,128)(2,1)S(1)} %get-tuple-element.23), channel_id=1, source_target_pairs={{0,1},{1,0},{2,3},{3,2},{4,5},{5,4},{6,7},{7,6},{8,9},{9,8},{10,11... | collective-permute-start | bytes 786440 | tf_op jit(solution)/shard_map/ppermute | solution.py:192
  25.2 11.1 %local.2 = (f32[2048,1024]{1,0:T(8,128)}, f32[4,16,128]{2,1,0:T(8,128)S(1)}) custom-call(bf16[128,1024]{1,0:T(8,128)(2,1)S(1)} %get-tuple-element.14.refs_0_, bf16[128,1024]{1,0:T(8,128)(2,1)S(1)} %collective-permute-done.6.refs_1_, bf16[128,1024]{1,0:T(8,128)(2,1)S(1)} %collective-permute-done.7.refs_2_, ...), custom_call_target="tpu_custom_call" | custom-call | flops 3221225472 | bytes 8388608 | tf_op jit(solution)/shard_map/local/pallas_call | solution.py:209
  36.3 1.5 %collective-permute-start.19 = (s32[8,16,128]{2,1,0:T(8,128)S(1)}, s32[8,16,128]{2,1,0:T(8,128)S(1)}, u32[]{:S(2)}, u32[]{:S(2)}) collective-permute-start(s32[8,16,128]{2,1,0:T(8,128)S(1)} %reshape_squeeze.3.refs_9_.refs_8_), channel_id=1, source_target_pairs={{0,4},{4,0},{8,12},{12,8},{16,20},{20,16},{24,28},{28,24},{1,5},{5... | collective-permute-start | bytes 196616 | tf_op jit(solution)/shard_map/ppermute | solution.py:192
  38.3 1.5 %collective-permute-start.21 = (s32[8,16,128]{2,1,0:T(8,128)S(1)}, s32[8,16,128]{2,1,0:T(8,128)S(1)}, u32[]{:S(2)}, u32[]{:S(2)}) collective-permute-start(s32[8,16,128]{2,1,0:T(8,128)S(1)} %collective-permute-done.17.refs_10_), channel_id=1, source_target_pairs={{0,4},{4,0},{8,12},{12,8},{16,20},{20,16},{24,28},{28,24},{1,5},{5... | collective-permute-start | bytes 196616 | tf_op jit(solution)/shard_map/ppermute | solution.py:192
  40.4 11.1 %local.3 = (f32[2048,1024]{1,0:T(8,128)}, f32[4,16,128]{2,1,0:T(8,128)S(1)}) custom-call(bf16[128,1024]{1,0:T(8,128)(2,1)S(1)} %get-tuple-element.24.refs_0_, bf16[128,1024]{1,0:T(8,128)(2,1)S(1)} %collective-permute-done.refs_1_, bf16[128,1024]{1,0:T(8,128)(2,1)S(1)} %collective-permute-done.1.refs_2_, ...), custom_call_target="tpu_custom_call", output_to_operand_aliasing={{0}: (11, {})} | custom-call | flops 3221225472 | bytes 8388608 | tf_op jit(solution)/shard_map/local/pallas_call | solution.py:209
  51.5 2.9 %collective-permute-start.11 = (f32[4,16,128]{2,1,0:T(8,128)S(1)}, f32[4,16,128]{2,1,0:T(8,128)S(1)}, u32[]{:S(2)}, u32[]{:S(2)}) collective-permute-start(f32[4,16,128]{2,1,0:T(8,128)S(1)} %get-tuple-element.20.refs_0_), channel_id=1, source_target_pairs={{0,24},{4,28},{8,16},{12,20},{16,8},{20,12},{24,0},{28,4},{1,25},{... | collective-permute-start | bytes 98312 | tf_op jit(solution)/shard_map/ppermute | solution.py:192
  54.4 1.9 %collective-permute-start.25 = (f32[4,16,128]{2,1,0:T(8,128)S(1)}, f32[4,16,128]{2,1,0:T(8,128)S(1)}, u32[]{:S(2)}, u32[]{:S(2)}) collective-permute-start(f32[4,16,128]{2,1,0:T(8,128)S(1)} %get-tuple-element.21.refs_0_), channel_id=1, source_target_pairs={{0,24},{4,28},{8,16},{12,20},{16,8},{20,12},{24,0},{28,4},{1,25},{... | collective-permute-start | bytes 98312 | tf_op jit(solution)/shard_map/ppermute | solution.py:192
  56.3 1.1 %collective-permute-start.24 = (f32[4,16,128]{2,1,0:T(8,128)S(1)}, f32[4,16,128]{2,1,0:T(8,128)S(1)}, u32[]{:S(2)}, u32[]{:S(2)}) collective-permute-start(f32[4,16,128]{2,1,0:T(8,128)S(1)} %get-tuple-element.21.refs_0_), channel_id=1, source_target_pairs={{0,16},{4,20},{8,24},{12,28},{16,0},{20,4},{24,8},{28,12},{1,17},{... | collective-permute-start | bytes 98312 | tf_op jit(solution)/shard_map/ppermute | solution.py:192
  57.4 1.5 %collective-permute-start.23 = (f32[4,16,128]{2,1,0:T(8,128)S(1)}, f32[4,16,128]{2,1,0:T(8,128)S(1)}, u32[]{:S(2)}, u32[]{:S(2)}) collective-permute-start(f32[4,16,128]{2,1,0:T(8,128)S(1)} %get-tuple-element.21.refs_0_), channel_id=1, source_target_pairs={{0,8},{4,12},{8,0},{12,4},{16,24},{20,28},{24,16},{28,20},{1,9},{5... | collective-permute-start | bytes 98312 | tf_op jit(solution)/shard_map/ppermute | solution.py:192
  59.4 1.5 %collective-permute-start.26 = (f32[4,16,128]{2,1,0:T(8,128)S(1)}, f32[4,16,128]{2,1,0:T(8,128)S(1)}, u32[]{:S(2)}, u32[]{:S(2)}) collective-permute-start(f32[4,16,128]{2,1,0:T(8,128)S(1)} %get-tuple-element.21.refs_0_), channel_id=1, source_target_pairs={{0,4},{4,0},{8,12},{12,8},{16,20},{20,16},{24,28},{28,24},{1,5},{5... | collective-permute-start | bytes 98312 | tf_op jit(solution)/shard_map/ppermute | solution.py:192
  61.8 1.2 %collective-permute-start.28 = (f32[4,16,128]{2,1,0:T(8,128)S(1)}, f32[4,16,128]{2,1,0:T(8,128)S(1)}, u32[]{:S(2)}, u32[]{:S(2)}) collective-permute-start(f32[4,16,128]{2,1,0:T(8,128)S(1)} %collective-permute-done.24.refs_2_), channel_id=1, source_target_pairs={{0,4},{4,0},{8,12},{12,8},{16,20},{20,16},{24,28},{28,24},{1,5},{5... | collective-permute-start | bytes 98312 | tf_op jit(solution)/shard_map/ppermute | solution.py:192
  63.8 1.2 %collective-permute-start.12 = (f32[4,16,128]{2,1,0:T(8,128)S(1)}, f32[4,16,128]{2,1,0:T(8,128)S(1)}, u32[]{:S(2)}, u32[]{:S(2)}) collective-permute-start(f32[4,16,128]{2,1,0:T(8,128)S(1)} %get-tuple-element.20.refs_0_), channel_id=1, source_target_pairs={{0,4},{4,0},{8,12},{12,8},{16,20},{20,16},{24,28},{28,24},{1,5},{5... | collective-permute-start | bytes 98312 | tf_op jit(solution)/shard_map/ppermute | solution.py:192
  65.8 1.2 %collective-permute-start.14 = (f32[4,16,128]{2,1,0:T(8,128)S(1)}, f32[4,16,128]{2,1,0:T(8,128)S(1)}, u32[]{:S(2)}, u32[]{:S(2)}) collective-permute-start(f32[4,16,128]{2,1,0:T(8,128)S(1)} %collective-permute-done.10.refs_2_), channel_id=1, source_target_pairs={{0,4},{4,0},{8,12},{12,8},{16,20},{20,16},{24,28},{28,24},{1,5},{5... | collective-permute-start | bytes 98312 | tf_op jit(solution)/shard_map/ppermute | solution.py:192
  67.9 9.5 %shared.2.refs_17_ = f32[2048,1024]{1,0:T(8,128)} custom-call(f32[4,16,128]{2,1,0:T(8,128)S(1)} %get-tuple-element.21.refs_0_, f32[4,16,128]{2,1,0:T(8,128)S(1)} %collective-permute-done.23.refs_1_, f32[4,16,128]{2,1,0:T(8,128)S(1)} %collective-permute-done.24.refs_2_, f32[4,16,128]{2,1,0:T(8,128)S(1)} %collective-permute-done.25.refs_3_, ...), custom_call_target="tpu_custom_call" | custom-call | flops 3221225472 | bytes 4194304 | tf_op jit(solution)/shard_map/shared/pallas_call | solution.py:245
  77.4 9.5 %shared.3 = f32[2048,1024]{1,0:T(8,128)} custom-call(f32[4,16,128]{2,1,0:T(8,128)S(1)} %get-tuple-element.20.refs_0_, f32[4,16,128]{2,1,0:T(8,128)S(1)} %collective-permute-done.9.refs_1_, f32[4,16,128]{2,1,0:T(8,128)S(1)} %collective-permute-done.10.refs_2_, f32[4,16,128]{2,1,0:T(8,128)S(1)} %collective-permute-done.11.refs_3_, ...), custom_call_target="tpu_custom_call", output_to_operand_aliasing={{}: (17, {})} | custom-call | flops 3221225472 | bytes 4194304 | tf_op jit(solution)/shard_map/shared/pallas_call | solution.py:245
  (46 shorter events, 10.1 us)
Async XLA Ops:
  0.6 14.7 %collective-permute-start.3 = (bf16[128,1024]{1,0:T(8,128)(2,1)}, bf16[128,1024]{1,0:T(8,128)(2,1)S(1)}, u32[]{:S(2)}, u32[]{:S(2)}) collective-permute-start(bf16[128,1024]{1,0:T(8,128)(2,1)} %bitcast.23), channel_id=1, source_target_pairs={{0,1},{1,0},{2,3},{3,2},{4,5},{5,4},{6,7},{7,6},{8,9},{9,8},{10,11... | collective-permute-start | bytes 786440 | tf_op jit(solution)/shard_map/ppermute | solution.py:192
  1.2 11.7 %collective-permute-start.4 = (bf16[128,1024]{1,0:T(8,128)(2,1)}, bf16[128,1024]{1,0:T(8,128)(2,1)S(1)}, u32[]{:S(2)}, u32[]{:S(2)}) collective-permute-start(bf16[128,1024]{1,0:T(8,128)(2,1)} %bitcast.24), channel_id=1, source_target_pairs={{0,2},{1,3},{2,0},{3,1},{4,6},{5,7},{6,4},{7,5},{8,10},{9,11},{10,... | collective-permute-start | bytes 786440 | tf_op jit(solution)/shard_map/ppermute | solution.py:192
  6.1 6.2 %collective-permute-start.18 = (s32[8,16,128]{2,1,0:T(8,128)S(1)}, s32[8,16,128]{2,1,0:T(8,128)S(1)}, u32[]{:S(2)}, u32[]{:S(2)}) collective-permute-start(s32[8,16,128]{2,1,0:T(8,128)S(1)} %reshape_squeeze.3.refs_9_.refs_8_), channel_id=1, source_target_pairs={{0,24},{4,28},{8,16},{12,20},{16,8},{20,12},{24,0},{28,4},{1,25},{... | collective-permute-start | bytes 196616 | tf_op jit(solution)/shard_map/ppermute | solution.py:192
  9.8 6.8 %collective-permute-start.6 = (bf16[128,1024]{1,0:T(8,128)(2,1)S(1)}, bf16[128,1024]{1,0:T(8,128)(2,1)S(1)}, u32[]{:S(2)}, u32[]{:S(2)}) collective-permute-start(bf16[128,1024]{1,0:T(8,128)(2,1)S(1)} %get-tuple-element.15), channel_id=1, source_target_pairs={{0,1},{1,0},{2,3},{3,2},{4,5},{5,4},{6,7},{7,6},{8,9},{9,8},{10,11... | collective-permute-start | bytes 786440 | tf_op jit(solution)/shard_map/ppermute | solution.py:192
  9.8 9.6 %collective-permute-start.7 = (bf16[128,1024]{1,0:T(8,128)(2,1)S(1)}, bf16[128,1024]{1,0:T(8,128)(2,1)S(1)}, u32[]{:S(2)}, u32[]{:S(2)}) collective-permute-start(bf16[128,1024]{1,0:T(8,128)(2,1)S(1)} %get-tuple-element.16), channel_id=1, source_target_pairs={{0,2},{1,3},{2,0},{3,1},{4,6},{5,7},{6,4},{7,5},{8,10},{9,11},{10,... | collective-permute-start | bytes 786440 | tf_op jit(solution)/shard_map/ppermute | solution.py:192
  12.3 11.4 %collective-permute-start.8 = (bf16[128,1024]{1,0:T(8,128)(2,1)S(1)}, bf16[128,1024]{1,0:T(8,128)(2,1)S(1)}, u32[]{:S(2)}, u32[]{:S(2)}) collective-permute-start(bf16[128,1024]{1,0:T(8,128)(2,1)S(1)} %get-tuple-element.17), channel_id=1, source_target_pairs={{0,3},{1,2},{2,1},{3,0},{4,7},{5,6},{6,5},{7,4},{8,11},{9,10},{10,... | collective-permute-start | bytes 786440 | tf_op jit(solution)/shard_map/ppermute | solution.py:192
  12.9 11.9 %collective-permute-start.5 = (bf16[128,1024]{1,0:T(8,128)(2,1)S(1)}, bf16[128,1024]{1,0:T(8,128)(2,1)S(1)}, u32[]{:S(2)}, u32[]{:S(2)}) collective-permute-start(bf16[128,1024]{1,0:T(8,128)(2,1)S(1)} %collective-permute-done.4.refs_6_), channel_id=1, source_target_pairs={{0,1},{1,0},{2,3},{3,2},{4,5},{5,4},{6,7},{7,6},{8,9},{9,8},{10,11... | collective-permute-start | bytes 786440 | tf_op jit(solution)/shard_map/ppermute | solution.py:192
  15.4 20.9 %collective-permute-start.17 = (s32[8,16,128]{2,1,0:T(8,128)S(1)}, s32[8,16,128]{2,1,0:T(8,128)S(1)}, u32[]{:S(2)}, u32[]{:S(2)}) collective-permute-start(s32[8,16,128]{2,1,0:T(8,128)S(1)} %reshape_squeeze.3.refs_9_.refs_8_), channel_id=1, source_target_pairs={{0,16},{4,20},{8,24},{12,28},{16,0},{20,4},{24,8},{28,12},{1,17},{... | collective-permute-start | bytes 196616 | tf_op jit(solution)/shard_map/ppermute | solution.py:192
  16.6 21.3 %collective-permute-start.16 = (s32[8,16,128]{2,1,0:T(8,128)S(1)}, s32[8,16,128]{2,1,0:T(8,128)S(1)}, u32[]{:S(2)}, u32[]{:S(2)}) collective-permute-start(s32[8,16,128]{2,1,0:T(8,128)S(1)} %reshape_squeeze.3.refs_9_.refs_8_), channel_id=1, source_target_pairs={{0,8},{4,12},{8,0},{12,4},{16,24},{20,28},{24,16},{28,20},{1,9},{5... | collective-permute-start | bytes 196616 | tf_op jit(solution)/shard_map/ppermute | solution.py:192
  19.4 19.0 %collective-permute-start.2 = (bf16[128,1024]{1,0:T(8,128)(2,1)S(1)}, bf16[128,1024]{1,0:T(8,128)(2,1)S(1)}, u32[]{:S(2)}, u32[]{:S(2)}) collective-permute-start(bf16[128,1024]{1,0:T(8,128)(2,1)S(1)} %get-tuple-element.22), channel_id=1, source_target_pairs={{0,3},{1,2},{2,1},{3,0},{4,7},{5,6},{6,5},{7,4},{8,11},{9,10},{10,... | collective-permute-start | bytes 786440 | tf_op jit(solution)/shard_map/ppermute | solution.py:192
  23.7 16.2 %collective-permute-start = (bf16[128,1024]{1,0:T(8,128)(2,1)S(1)}, bf16[128,1024]{1,0:T(8,128)(2,1)S(1)}, u32[]{:S(2)}, u32[]{:S(2)}) collective-permute-start(bf16[128,1024]{1,0:T(8,128)(2,1)S(1)} %get-tuple-element.23), channel_id=1, source_target_pairs={{0,1},{1,0},{2,3},{3,2},{4,5},{5,4},{6,7},{7,6},{8,9},{9,8},{10,11... | collective-permute-start | bytes 786440 | tf_op jit(solution)/shard_map/ppermute | solution.py:192
  24.7 15.7 %collective-permute-start.1 = (bf16[128,1024]{1,0:T(8,128)(2,1)S(1)}, bf16[128,1024]{1,0:T(8,128)(2,1)S(1)}, u32[]{:S(2)}, u32[]{:S(2)}) collective-permute-start(bf16[128,1024]{1,0:T(8,128)(2,1)S(1)} %get-tuple-element.25), channel_id=1, source_target_pairs={{0,2},{1,3},{2,0},{3,1},{4,6},{5,7},{6,4},{7,5},{8,10},{9,11},{10,... | collective-permute-start | bytes 786440 | tf_op jit(solution)/shard_map/ppermute | solution.py:192
  36.3 18.1 %collective-permute-start.19 = (s32[8,16,128]{2,1,0:T(8,128)S(1)}, s32[8,16,128]{2,1,0:T(8,128)S(1)}, u32[]{:S(2)}, u32[]{:S(2)}) collective-permute-start(s32[8,16,128]{2,1,0:T(8,128)S(1)} %reshape_squeeze.3.refs_9_.refs_8_), channel_id=1, source_target_pairs={{0,4},{4,0},{8,12},{12,8},{16,20},{20,16},{24,28},{28,24},{1,5},{5... | collective-permute-start | bytes 196616 | tf_op jit(solution)/shard_map/ppermute | solution.py:192
  37.8 16.6 %collective-permute-start.22 = (s32[8,16,128]{2,1,0:T(8,128)S(1)}, s32[8,16,128]{2,1,0:T(8,128)S(1)}, u32[]{:S(2)}, u32[]{:S(2)}) collective-permute-start(s32[8,16,128]{2,1,0:T(8,128)S(1)} %collective-permute-done.18.refs_11_), channel_id=1, source_target_pairs={{0,4},{4,0},{8,12},{12,8},{16,20},{20,16},{24,28},{28,24},{1,5},{5... | collective-permute-start | bytes 196616 | tf_op jit(solution)/shard_map/ppermute | solution.py:192
  38.3 17.9 %collective-permute-start.21 = (s32[8,16,128]{2,1,0:T(8,128)S(1)}, s32[8,16,128]{2,1,0:T(8,128)S(1)}, u32[]{:S(2)}, u32[]{:S(2)}) collective-permute-start(s32[8,16,128]{2,1,0:T(8,128)S(1)} %collective-permute-done.17.refs_10_), channel_id=1, source_target_pairs={{0,4},{4,0},{8,12},{12,8},{16,20},{20,16},{24,28},{28,24},{1,5},{5... | collective-permute-start | bytes 196616 | tf_op jit(solution)/shard_map/ppermute | solution.py:192
  39.8 17.5 %collective-permute-start.20 = (s32[8,16,128]{2,1,0:T(8,128)S(1)}, s32[8,16,128]{2,1,0:T(8,128)S(1)}, u32[]{:S(2)}, u32[]{:S(2)}) collective-permute-start(s32[8,16,128]{2,1,0:T(8,128)S(1)} %collective-permute-done.16.refs_9_), channel_id=1, source_target_pairs={{0,4},{4,0},{8,12},{12,8},{16,20},{20,16},{24,28},{28,24},{1,5},{5... | collective-permute-start | bytes 196616 | tf_op jit(solution)/shard_map/ppermute | solution.py:192
  51.5 7.4 %collective-permute-start.11 = (f32[4,16,128]{2,1,0:T(8,128)S(1)}, f32[4,16,128]{2,1,0:T(8,128)S(1)}, u32[]{:S(2)}, u32[]{:S(2)}) collective-permute-start(f32[4,16,128]{2,1,0:T(8,128)S(1)} %get-tuple-element.20.refs_0_), channel_id=1, source_target_pairs={{0,24},{4,28},{8,16},{12,20},{16,8},{20,12},{24,0},{28,4},{1,25},{... | collective-permute-start | bytes 98312 | tf_op jit(solution)/shard_map/ppermute | solution.py:192
  54.4 6.5 %collective-permute-start.25 = (f32[4,16,128]{2,1,0:T(8,128)S(1)}, f32[4,16,128]{2,1,0:T(8,128)S(1)}, u32[]{:S(2)}, u32[]{:S(2)}) collective-permute-start(f32[4,16,128]{2,1,0:T(8,128)S(1)} %get-tuple-element.21.refs_0_), channel_id=1, source_target_pairs={{0,24},{4,28},{8,16},{12,20},{16,8},{20,12},{24,0},{28,4},{1,25},{... | collective-permute-start | bytes 98312 | tf_op jit(solution)/shard_map/ppermute | solution.py:192
  57.4 5.6 %collective-permute-start.23 = (f32[4,16,128]{2,1,0:T(8,128)S(1)}, f32[4,16,128]{2,1,0:T(8,128)S(1)}, u32[]{:S(2)}, u32[]{:S(2)}) collective-permute-start(f32[4,16,128]{2,1,0:T(8,128)S(1)} %get-tuple-element.21.refs_0_), channel_id=1, source_target_pairs={{0,8},{4,12},{8,0},{12,4},{16,24},{20,28},{24,16},{28,20},{1,9},{5... | collective-permute-start | bytes 98312 | tf_op jit(solution)/shard_map/ppermute | solution.py:192
  59.4 5.6 %collective-permute-start.26 = (f32[4,16,128]{2,1,0:T(8,128)S(1)}, f32[4,16,128]{2,1,0:T(8,128)S(1)}, u32[]{:S(2)}, u32[]{:S(2)}) collective-permute-start(f32[4,16,128]{2,1,0:T(8,128)S(1)} %get-tuple-element.21.refs_0_), channel_id=1, source_target_pairs={{0,4},{4,0},{8,12},{12,8},{16,20},{20,16},{24,28},{28,24},{1,5},{5... | collective-permute-start | bytes 98312 | tf_op jit(solution)/shard_map/ppermute | solution.py:192
  63.8 13.6 %collective-permute-start.12 = (f32[4,16,128]{2,1,0:T(8,128)S(1)}, f32[4,16,128]{2,1,0:T(8,128)S(1)}, u32[]{:S(2)}, u32[]{:S(2)}) collective-permute-start(f32[4,16,128]{2,1,0:T(8,128)S(1)} %get-tuple-element.20.refs_0_), channel_id=1, source_target_pairs={{0,4},{4,0},{8,12},{12,8},{16,20},{20,16},{24,28},{28,24},{1,5},{5... | collective-permute-start | bytes 98312 | tf_op jit(solution)/shard_map/ppermute | solution.py:192
  65.0 12.4 %collective-permute-start.15 = (f32[4,16,128]{2,1,0:T(8,128)S(1)}, f32[4,16,128]{2,1,0:T(8,128)S(1)}, u32[]{:S(2)}, u32[]{:S(2)}) collective-permute-start(f32[4,16,128]{2,1,0:T(8,128)S(1)} %collective-permute-done.11.refs_3_), channel_id=1, source_target_pairs={{0,4},{4,0},{8,12},{12,8},{16,20},{20,16},{24,28},{28,24},{1,5},{5... | collective-permute-start | bytes 98312 | tf_op jit(solution)/shard_map/ppermute | solution.py:192
  65.8 11.5 %collective-permute-start.14 = (f32[4,16,128]{2,1,0:T(8,128)S(1)}, f32[4,16,128]{2,1,0:T(8,128)S(1)}, u32[]{:S(2)}, u32[]{:S(2)}) collective-permute-start(f32[4,16,128]{2,1,0:T(8,128)S(1)} %collective-permute-done.10.refs_2_), channel_id=1, source_target_pairs={{0,4},{4,0},{8,12},{12,8},{16,20},{20,16},{24,28},{28,24},{1,5},{5... | collective-permute-start | bytes 98312 | tf_op jit(solution)/shard_map/ppermute | solution.py:192
  67.0 10.4 %collective-permute-start.13 = (f32[4,16,128]{2,1,0:T(8,128)S(1)}, f32[4,16,128]{2,1,0:T(8,128)S(1)}, u32[]{:S(2)}, u32[]{:S(2)}) collective-permute-start(f32[4,16,128]{2,1,0:T(8,128)S(1)} %collective-permute-done.9.refs_1_), channel_id=1, source_target_pairs={{0,4},{4,0},{8,12},{12,8},{16,20},{20,16},{24,28},{28,24},{1,5},{5... | collective-permute-start | bytes 98312 | tf_op jit(solution)/shard_map/ppermute | solution.py:192
  (6 other events, 30.6 us)

commit v2 on v1

v2 whole, which is shorter than its diff:
```python
import functools

import jax
import jax.numpy as jnp
import numpy as np
from jax import lax
from jax.experimental import pallas as pl
from jax.experimental.pallas import tpu as pltpu
from jax.sharding import PartitionSpec as P

GROUP = 64
LANES = 128
WIDE = 256


FACTORS = tuple(1.0 + k / 128.0 for k in (1, 2, 10, 15, 24, 25, 28, 61, 74, 82, 94, 97, 98, 107, 113))
PARTS = 2

momentum_decay = 0.999
sharpness = 4.0


def dct_table(extent):
    frequency = np.arange(extent, dtype=np.float64)[:, None]
    location = np.arange(extent, dtype=np.float64)[None, :]
    cosines = np.cos(np.pi * (2.0 * location + 1.0) * frequency / (2.0 * extent))
    cosines = cosines * np.sqrt(2.0 / extent)
    cosines[0] *= np.sqrt(0.5)
    return cosines.astype(np.float32)


def bf16_parts(x):
    high = x.astype(jnp.bfloat16)
    return high, (x - high.astype(np.float32)).astype(jnp.bfloat16)


def forward_matrix(cosines):
    high, low = bf16_parts(np.kron(np.eye(WIDE // GROUP, dtype=np.float32), cosines.T))
    return np.concatenate([high, high, low], axis=0)


def side_matrix(cosines):
    high, low = bf16_parts(cosines.T)
    return np.concatenate([high, high, low, low], axis=1)


def right_matrix(cosines):
    high, low = bf16_parts(np.kron(np.eye(LANES // GROUP, dtype=np.float32), cosines))
    upper = np.concatenate([high, low], axis=1)
    return np.concatenate([upper, np.concatenate([high, np.zeros_like(low)], axis=1)], axis=0)


def all_matrices(cosines):
    parts = [forward_matrix(cosines), right_matrix(cosines), side_matrix(cosines)]
    return np.concatenate(parts, axis=0)


FORWARD = slice(0, 3 * WIDE)
RIGHT = slice(3 * WIDE, 4 * WIDE)
SIDE = slice(4 * WIDE, 4 * WIDE + GROUP)


def halves(x):
    high = x.astype(jnp.bfloat16)
    return high, (x - high.astype(jnp.float32)).astype(jnp.bfloat16)


def nt_dot(a, b):
    return lax.dot_general(a, b, (((1,), (1,)), ((), ())), preferred_element_type=jnp.float32)


def right_product(x, stacked):
    high, low = halves(x)
    return jnp.dot(
        jnp.concatenate([high, low, high], axis=1), stacked, preferred_element_type=jnp.float32
    )


def local_kernel(sources, kept, *refs):
    token_refs, upstream_refs = refs[:sources], refs[sources : 2 * sources]
    moment_ref, spot_ref, matrix_ref = refs[2 * sources : 2 * sources + 3]
    next_ref, message_ref, half_ref, scaled_ref, base_ref, value_ref = refs[-6:]
    rows, cols = moment_ref.shape
    per_row = LANES // kept
    lane = lax.broadcasted_iota(jnp.int32, (8, LANES), 1)
    first = lane < 2 * kept
    shift = GROUP * ((lane // kept) % 2)
    side = matrix_ref[SIDE, :].astype(jnp.float32)
    side = side[:, :LANES] + side[:, LANES:]
    table = [side[8 * k : 8 * k + 8, :] for k in range(GROUP // 8)]
    lane_group = lax.broadcasted_iota(jnp.int32, (WIDE, LANES), 1) // kept
    row_group = lax.broadcasted_iota(jnp.int32, (WIDE, LANES), 0) // GROUP
    lane_wide = lax.broadcasted_iota(jnp.int32, (GROUP, 2 * LANES), 1) % LANES // kept
    zero = jnp.zeros((), jnp.bfloat16)
    gradient = lax.dot_general(
        jnp.concatenate([r[...] for r in token_refs], axis=0),
        jnp.concatenate([r[...] for r in upstream_refs], axis=0),
        (((0,), (0,)), ((), ())),
        preferred_element_type=jnp.float32,
    )
    next_ref[...] = momentum_decay * moment_ref[...] + gradient
    for c in range(cols // WIDE):
        span = slice(c * WIDE, c * WIDE + WIDE)
        half_ref[:, span] = right_product(next_ref[:, span], matrix_ref[FORWARD, :])
    for p in range(rows // GROUP):
        for c in range(cols // WIDE):
            at = p * (cols // WIDE) + c
            spots = jnp.broadcast_to(spot_ref[0, at : at + 1, :], (8, LANES))
            upper, lower = spots // GROUP, spots % GROUP
            where = lower + shift
            total = jnp.zeros((8, LANES), jnp.float32)
            starts = [p * GROUP + 8 * k for k in range(GROUP // 8)]
            low_span = slice(c * WIDE, c * WIDE + LANES)
            high_span = slice(c * WIDE + LANES, c * WIDE + WIDE)
            ones = [jnp.take_along_axis(half_ref[b : b + 8, low_span], where, axis=1) for b in starts]
            twos = [jnp.take_along_axis(half_ref[b : b + 8, high_span], where, axis=1) for b in starts]
            upper_rows = [jnp.take_along_axis(t, upper, axis=1) for t in table]
            lower_rows = [jnp.take_along_axis(t, lower, axis=1) for t in table]
            for one, two, up in zip(ones, twos, upper_rows):
                total = total + jnp.where(first, one, two) * up
            value = jnp.sum(total, axis=0, keepdims=True)
            value_ref[at : at + 1, :] = value
            s_high, s_low = halves(jnp.concatenate(upper_rows, axis=0) * value)
            b_high, b_low = halves(jnp.concatenate(lower_rows, axis=0))
            scaled_ref[at] = jnp.concatenate([s_high, s_low], axis=1)
            base_ref[at] = jnp.concatenate([b_high, b_low], axis=1)
    for p in range(rows // GROUP):
        for c in range(cols // WIDE):
            at = p * (cols // WIDE) + c
            scaled, base = scaled_ref[at], base_ref[at]
            b_high, b_low = base[:, :LANES], base[:, LANES:]
            b_high = jnp.concatenate([b_high, b_high], axis=1)
            b_low = jnp.concatenate([b_low, b_low], axis=1)
            masked = [jnp.where(lane_wide == a, scaled, zero) for a in range(per_row)]
            prod = nt_dot(
                jnp.concatenate(masked, axis=0),
                jnp.concatenate([b_high, b_high, b_low, b_low], axis=0),
            )
            prod = prod[:, :LANES] + prod[:, LANES:]
            left = lax.broadcasted_iota(jnp.int32, (GROUP, LANES), 1) < GROUP
            own = jnp.concatenate([jnp.where(left, prod[2 * b * GROUP : 2 * b * GROUP + GROUP], prod[2 * b * GROUP + GROUP : 2 * b * GROUP + 2 * GROUP]) for b in range(per_row // 2)], axis=1)
            block, span = slice(p * GROUP, p * GROUP + GROUP), slice(c * WIDE, c * WIDE + WIDE)
            next_ref[block, span] = next_ref[block, span] - own
    for n, part in enumerate(as_product(value_ref[...])):
        part = part.astype(jnp.bfloat16)
        for j in range(message_ref.shape[0]):
            message_ref[j, 0, n] = part


def as_product(value):
    best = value.astype(jnp.bfloat16).astype(jnp.float32)
    factor = jnp.ones_like(value)
    error = jnp.abs(best - value)
    for b in FACTORS:
        a = (value * (1.0 / b)).astype(jnp.bfloat16).astype(jnp.float32)
        trial = jnp.abs(a * b - value)
        better = trial < error
        error = jnp.where(better, trial, error)
        best = jnp.where(better, a, best)
        factor = jnp.where(better, b, factor)
    return best, factor


def shared_kernel(kept, *refs):
    message_ref, spot_ref, matrix_ref = refs[:3]
    step_ref, dense_ref = refs[-2:]
    replicas = message_ref.shape[0]
    depth = replicas * kept
    rows, cols = step_ref.shape
    per_row = LANES // kept
    level = lax.broadcasted_iota(jnp.int32, (GROUP, depth), 0)
    level = level.astype(jnp.float32).astype(jnp.bfloat16)
    zero = jnp.zeros((), jnp.bfloat16)

    def filled(x, at):
        tile = jnp.broadcast_to(x[at : at + 1], (16, depth)).astype(jnp.bfloat16)
        return jnp.concatenate([tile] * (GROUP // 16), axis=0)

    parts = [
        [message_ref[j, 0, n].astype(jnp.float32) for j in range(replicas)] for n in range(PARTS)
    ]
    parts.append([spot_ref[j, 0].astype(jnp.int32) for j in range(replicas)])
    for a in range(per_row):
        span = slice(a * kept, a * kept + kept)
        best, factor, place = [jnp.concatenate([x[:, span] for x in p], axis=1) for p in parts]
        upper = (place // GROUP).astype(jnp.float32)
        lower = (place % GROUP).astype(jnp.float32)
        for at in range(best.shape[0]):
            p, c = at // (cols // WIDE), at % (cols // WIDE)
            hot_upper = jnp.where(level == filled(upper, at), filled(factor, at), zero)
            hot_lower = jnp.where(level == filled(lower, at), filled(best, at), zero)
            place = slice(c * WIDE + a * GROUP, c * WIDE + a * GROUP + GROUP)
            dense_ref[p * GROUP : p * GROUP + GROUP, place] = nt_dot(hot_upper, hot_lower)
    pieces = []
    for c in range(cols // WIDE):
        parts = []
        for p in range(rows // GROUP):
            tile = dense_ref[p * GROUP : p * GROUP + GROUP, c * WIDE : c * WIDE + WIDE]
            high, low = halves(tile)
            stack = jnp.concatenate([high, low, high], axis=0)
            parts.append(jnp.dot(matrix_ref[SIDE, : 3 * GROUP], stack, preferred_element_type=jnp.float32))
        high, low = halves(jnp.concatenate(parts, axis=0))
        for b in range(WIDE // LANES):
            span = slice(b * LANES, b * LANES + LANES)
            pieces.append(jnp.concatenate([high[:, span], low[:, span]], axis=1))
    product = jnp.dot(
        jnp.concatenate(pieces, axis=0), matrix_ref[RIGHT, :], preferred_element_type=jnp.float32
    )
    for b in range(len(pieces)):
        part = product[b * rows : b * rows + rows]
        update = part[:, :LANES] + part[:, LANES:]
        step_ref[:, b * LANES : b * LANES + LANES] = jnp.tanh(sharpness * update)


def swap(x, axis, count, offset):
    return lax.ppermute(x, axis, [(i, i ^ offset) for i in range(count)])


def local_call(
    sources, kept, blocks, at, slot, columns, incoming, moment, spots, matrices, next_moment, message
):
    _, col_count = moment.shape
    tok = columns[0].shape[0]
    spot_rows = spots.shape[1]
    whole = pl.BlockSpec(memory_space=pltpu.VMEM)
    aliased, aliases = [], {}
    for position, array in enumerate((next_moment, message)):
        if not isinstance(array, jax.ShapeDtypeStruct):
            aliases[2 * sources + 3 + len(aliased)] = position
            aliased.append(array)
    rows = blocks * WIDE
    return pl.pallas_call(
        functools.partial(local_kernel, sources, kept),
        grid=(blocks,),
        in_specs=[pl.BlockSpec((tok, WIDE), lambda i: (0, i))] * sources
        + [whole] * sources
        + [
            pl.BlockSpec((WIDE, col_count), lambda i: (at + i, 0)),
            pl.BlockSpec((1, spot_rows, LANES), lambda i: (at + i, 0, 0)),
            whole,
        ]
        + [pl.BlockSpec(memory_space=pl.ANY)] * len(aliased),
        out_specs=[
            pl.BlockSpec((WIDE, col_count), lambda i: (at + i, 0)),
            pl.BlockSpec(
                (message.shape[0], 1) + message.shape[2:], lambda i: (0, slot + i, 0, 0, 0)
            ),
        ],
        out_shape=[jax.ShapeDtypeStruct(x.shape, x.dtype) for x in (next_moment, message)],
        input_output_aliases=aliases,
        scratch_shapes=[pltpu.VMEM((WIDE, col_count), jnp.float32)]
        + [pltpu.VMEM((spot_rows, GROUP, 2 * LANES), jnp.bfloat16)] * 2
        + [pltpu.VMEM((spot_rows, LANES), jnp.float32)],
        compiler_params=pltpu.CompilerParams(vmem_limit_bytes=48 * 2**20),
        cost_estimate=pl.CostEstimate(
            flops=12 * rows * col_count * WIDE, bytes_accessed=8 * rows * col_count, transcendentals=0
        ),
        name="local",
    )(*columns, *incoming, moment, spots, matrices, *aliased)


def shared_call(kept, blocks, at, shape, message, spots, matrices, previous):
    col_count = shape[1]
    whole = pl.BlockSpec(memory_space=pltpu.VMEM)
    aliased = [] if previous is None else [previous]
    rows = blocks * WIDE
    return pl.pallas_call(
        functools.partial(shared_kernel, kept),
        grid=(blocks,),
        in_specs=[
            pl.BlockSpec((message.shape[0], 1) + message.shape[2:], lambda i: (0, i, 0, 0, 0)),
            pl.BlockSpec((spots.shape[0], 1) + spots.shape[2:], lambda i: (0, at + i, 0, 0)),
            whole,
        ]
        + [pl.BlockSpec(memory_space=pl.ANY)] * len(aliased),
        out_specs=pl.BlockSpec((WIDE, col_count), lambda i: (at + i, 0)),
        out_shape=jax.ShapeDtypeStruct(shape, jnp.float32),
        input_output_aliases={3: 0} if aliased else {},
        scratch_shapes=[pltpu.VMEM((WIDE, col_count), jnp.float32)],
        compiler_params=pltpu.CompilerParams(vmem_limit_bytes=48 * 2**20),
        cost_estimate=pl.CostEstimate(
            flops=12 * rows * col_count * WIDE, bytes_accessed=4 * rows * col_count, transcendentals=0
        ),
        name="shared",
    )(message, spots, matrices, *aliased)


def chunk_sizes(steps):
    if steps < 4:
        return [1] * steps, [[k] for k in range(steps)]
    first = steps // 2
    return [first, steps - first], [[0], [1]]
    first = steps // 4
    second = (steps - first) // 2
    return [first, second, steps - first - second], [[0, 1], [2]]


def per_device(n_fsdp, n_rep, activations, cotangent, momentum, positions):
    tokens, upstream, moment = activations[0], cotangent[0], momentum[0]
    row_count, col_count = moment.shape
    kept = positions.shape[2]
    steps = row_count // WIDE
    sizes, travel = chunk_sizes(steps)
    starts = [sum(sizes[:k]) for k in range(len(sizes))]
    chunks = len(sizes)
    spot_rows = WIDE * col_count // (GROUP * GROUP) * kept // LANES
    me = lax.axis_index("fsdp")
    half = n_fsdp // 2

    def pieces_of(k, me):
        return [
            lax.dynamic_slice_in_dim(
                tokens, (me ^ offset) * row_count + starts[k] * WIDE, sizes[k] * WIDE, 1
            )
            for offset in range(n_fsdp)
        ]

    def exchange(pieces):
        out = [pieces[0]]
        for offset in range(1, n_fsdp):
            out.append(swap(pieces[offset], "fsdp", n_fsdp, offset))
        return out

    incoming = {0: upstream}
    offset = half
    while offset:
        for known in list(incoming):
            incoming[known ^ offset] = swap(incoming[known], "fsdp", n_fsdp, offset)
        offset //= 2
    pieces = pieces_of(0, me)
    me, positions, pieces = lax.optimization_barrier((me, positions, pieces))
    all_columns = [exchange(pieces)]
    for k in range(1, chunks):
        pieces = pieces_of(k, me)
        all_columns.append(exchange(pieces))
    spots = positions[0].reshape(steps, spot_rows, LANES)

    def settled(x):
        return jnp.where(me >= 0, x, jnp.zeros((), x.dtype))

    incoming = [settled(upstream)] + [incoming[i] for i in range(1, n_fsdp)]

    cosines = dct_table(GROUP)
    matrices = settled(all_matrices(cosines))

    copies = jnp.broadcast_to(spots.astype(jnp.int16)[None], (n_rep,) + spots.shape)
    all_spots = lax.all_to_all(copies, "rep", split_axis=0, concat_axis=0, tiled=True)
    next_moment = jax.ShapeDtypeStruct((row_count, col_count), jnp.float32)
    step, gathered = None, []
    for members in travel:
        blocks = sum(sizes[k] for k in members)
        message = jax.ShapeDtypeStruct((n_rep, blocks, PARTS, spot_rows, LANES), jnp.bfloat16)
        for k in members:
            next_moment, message = local_call(
                n_fsdp, kept, sizes[k], starts[k], starts[k] - starts[members[0]],
                all_columns[k], incoming, moment, spots, matrices, next_moment, message,
            )
        gathered.append(
            lax.all_to_all(message, "rep", split_axis=0, concat_axis=0, tiled=True)
        )
    for g, members in enumerate(travel):
        step = shared_call(
            kept, gathered[g].shape[1], starts[members[0]], moment.shape, gathered[g], all_spots,
            matrices, step,
        )
    return (next_moment[None], step)


def solution(mesh):
    spec = P("rep", "fsdp", None)
    return jax.shard_map(
        functools.partial(per_device, mesh.shape["fsdp"], mesh.shape["rep"]),
        mesh=mesh,
        in_specs=(spec, spec, spec, spec),
        out_specs=(spec, P("fsdp", None)),
        check_vma=False,
    )
```

time: 87.2 us -> 79.3 us (0.909)
  starting transfers between devices: 34.6 us -> 24.4 us
  Pallas kernels: 41.2 us -> 35.8 us
  local copies, waits for them, and re-layouts: 3.6 us -> 7.67 us
  waiting for transfers between devices: 4.68 us -> 7.95 us
    ppermute x30 -> x9, starting transfers between devices: 34.6 us -> 6.54 us  [swap(): return lax.ppermute(x, axis, [(i, i ^ offset) for i in range(count)])]
    all_to_all x0 -> x3, starting transfers between devices: none -> 17.9 us  [the longest x2 12.1 us: per_device(): lax.all_to_all(message, 'rep', split_axis=0, concat_axis=0, tiled=True)]
    pallas_call x2, Pallas kernels: 19 us -> 14.7 us  [shared_call(): pl.pallas_call(functools.partial(shared_kernel, kept), grid=(blocks,), in...]
    all_to_all x0 -> x3, waiting for transfers between devices: none -> 2.15 us  [the longest x2 2.15 us: per_device(): lax.all_to_all(message, 'rep', split_axis=0, concat_axis=0, tiled=True)]
    unnamed x0 -> x4, local copies, waits for them, and re-layouts: none -> 1.67 us
    dynamic_slice x2, local copies, waits for them, and re-layouts: 2.52 us -> 4.19 us  [pieces_of(): lax.dynamic_slice_in_dim(tokens, (me ^ offset) * row_count + starts[k] *...]
    ppermute x30 -> x9, waiting for transfers between devices: 4.68 us -> 5.8 us  [swap(): return lax.ppermute(x, axis, [(i, i ^ offset) for i in range(count)])]
    pallas_call x2, Pallas kernels: 22.2 us -> 21.1 us  [local_call(): pl.pallas_call(functools.partial(local_kernel, sources, kept), grid=(bloc...]
  transfers between devices with their start and end apart: 30 -> 12, of which waited for: 2 -> 3; matrix products, arithmetic and copies ran while one was open for 7% -> 10% of each run, Pallas kernels for 36% -> 36%
where the time goes in v2:
time: 79.3 us; the launch traced here: 78.6 us
  Pallas kernels  35.8 us (45%)
  starting transfers between devices  24.4 us (31%)
  waiting for transfers between devices  7.95 us (10%)
  local copies, waits for them, and re-layouts  7.67 us (10%)
  other arithmetic  2.07 us (3%)
    pallas_call x2, Pallas kernels, local_call(): pl.pallas_call(functools.partial(local_kernel, sources, kept), grid=(bloc...  21.1 us
    pallas_call x2, Pallas kernels, shared_call(): pl.pallas_call(functools.partial(shared_kernel, kept), grid=(blocks,), in...  14.7 us
    all_to_all x2, starting transfers between devices, per_device(): lax.all_to_all(message, 'rep', split_axis=0, concat_axis=0, tiled=True)  12.1 us
    ppermute x9, starting transfers between devices, swap(): return lax.ppermute(x, axis, [(i, i ^ offset) for i in range(count)])  6.54 us
    all_to_all x1, starting transfers between devices, per_device(): lax.all_to_all(copies, 'rep', split_axis=0, concat_axis=0, tiled=True)  5.81 us
    ppermute x9, waiting for transfers between devices, swap(): return lax.ppermute(x, axis, [(i, i ^ offset) for i in range(count)])  5.8 us
    dynamic_slice x2, local copies, waits for them, and re-layouts, pieces_of(): lax.dynamic_slice_in_dim(tokens, (me ^ offset) * row_count + starts[k] *...  4.19 us
    all_to_all x2, waiting for transfers between devices, per_device(): lax.all_to_all(message, 'rep', split_axis=0, concat_axis=0, tiled=True)  2.15 us
  transfers between devices with their start and end apart: 12, of which 3 were waited for; matrix products, arithmetic and copies ran while one was open for 10% of the time, Pallas kernels for 36%

profile of v2, /device:TPU:0, one launch (start us, length us, event | category | flops | bytes accessed | tf_op | source)
XLA Modules:
  0.0 78.6 jit_solution(16969044847942890744)
XLA Ops:
  0.6 0.6 collective-permute-start.3
  1.2 2.6 %collective-permute-start.4 = (bf16[128,1024]{1,0:T(8,128)(2,1)}, bf16[128,1024]{1,0:T(8,128)(2,1)S(1)}, u32[]{:S(2)}, u32[]{:S(2)}) collective-permute-start(bf16[128,1024]{1,0:T(8,128)(2,1)} %bitcast.24), channel_id=1, source_target_pairs={{0,2},{1,3},{2,0},{3,1},{4,6},{5,7},{6,4},{7,5},{8,10},{9,11},{10,... | collective-permute-start | bytes 786440 | tf_op jit(solution)/shard_map/ppermute | solution.py:216
  3.8 2.1 %dynamic-slice_bitcast_fusion.4 = (bf16[128,1024]{1,0:T(8,128)(2,1)}, bf16[128,1024]{1,0:T(8,128)(2,1)}, bf16[128,1024]{1,0:T(8,128)(2,1)S(1)}, bf16[128,1024]{1,0:T(8,128)(2,1)S(1)}) fusion(bf16[1,128,8192]{2,1,0:T(8,128)(2,1)} %param.5, s32[]{:T(128)S(6)} %select_n.43, s32[]{:T(128)S(6)} %select_n.42, s32[]{:T(128)S(6)} %select_n.41, s32[]{:T(128)S(6)} %select_n.40), kind=kLoop, calls=%fused_computation.5 | loop fusion | bytes 2097168 | tf_op jit(solution)/shard_map/dynamic_slice | solution.py:312
  5.9 1.0 %copy.10 = s32[1,512,32]{2,1,0:T(8,128)S(1)} copy(s32[1,512,32]{1,2,0:T(8,128)} %param.8) | data formatting | bytes 131072 | tf_op jit(solution)/shard_map/optimization_barrier | solution.py:331
  7.0 0.7 broadcast_in_dim.20
  7.7 5.8 %all-to-all-start.1 = ((s16[8,8,16,128]{3,2,1,0:T(8,128)(2,1)}), s16[8,8,16,128]{3,2,1,0:T(8,128)(2,1)S(1)}, u32[]{:S(2)}, u32[]{:S(2)}) async-start(s16[8,8,16,128]{3,2,1,0:T(8,128)(2,1)} %broadcast_in_dim.20), calls=%async_computation.1 | async-start | bytes 524288 | tf_op jit(solution)/shard_map/all_to_all | solution.py:347
  13.5 0.6 collective-permute-start.7
  14.1 1.3 %collective-permute-start.8 = (bf16[128,1024]{1,0:T(8,128)(2,1)}, bf16[128,1024]{1,0:T(8,128)(2,1)}, u32[]{:S(2)}, u32[]{:S(2)}) collective-permute-start(bf16[128,1024]{1,0:T(8,128)(2,1)} %get-tuple-element.17), channel_id=1, source_target_pairs={{0,3},{1,2},{2,1},{3,0},{4,7},{5,6},{6,5},{7,4},{8,11},{9,10},{10,... | collective-permute-start | bytes 786440 | tf_op jit(solution)/shard_map/ppermute | solution.py:216
  15.4 1.1 %broadcast_select_fusion.refs_10_.refs_2_ = bf16[1088,256]{1,0:T(8,128)(2,1)S(1)} fusion(bf16[1088,256]{1,0:T(8,128)(2,1)} %constant.35.clone, pred[]{:T(512)S(6)} %ge.4), kind=kLoop, calls=%fused_computation | loop fusion | flops 278528 | bytes 1114113 | tf_op jit(solution)/shard_map/jit(_where)/select_n | solution.py:339
  16.5 0.4 collective-permute-start.5
  16.9 1.0 %broadcast_select_fusion.1.refs_4_ = bf16[128,1024]{1,0:T(8,128)(2,1)S(1)} fusion(pred[]{:T(512)S(6)} %ge.4, bf16[1,128,1024]{2,1,0:T(8,128)(2,1)} %param.6), kind=kLoop, calls=%fused_computation.9 | loop fusion | flops 131072 | bytes 524289 | tf_op jit(solution)/shard_map/jit(_where)/select_n | solution.py:339
  17.9 2.1 %dynamic-slice_bitcast_fusion = (bf16[128,1024]{1,0:T(8,128)(2,1)}, bf16[128,1024]{1,0:T(8,128)(2,1)}, bf16[128,1024]{1,0:T(8,128)(2,1)S(1)}, bf16[128,1024]{1,0:T(8,128)(2,1)}) fusion(bf16[1,128,8192]{2,1,0:T(8,128)(2,1)} %param.5, s32[]{:T(128)S(6)} %select_n.47, s32[]{:T(128)S(6)} %select_n.45, s32[]{:T(128)S(6)} %select_n.44, s32[]{:T(128)S(6)} %select_n.46), kind=kLoop, calls=%fused_computation.1 | loop fusion | bytes 2097168 | tf_op jit(solution)/shard_map/dynamic_slice | solution.py:312
  20.6 2.4 %collective-permute-done.7.refs_2_ = bf16[128,1024]{1,0:T(8,128)(2,1)S(1)} collective-permute-done((bf16[128,1024]{1,0:T(8,128)(2,1)}, bf16[128,1024]{1,0:T(8,128)(2,1)S(1)}, u32[]{:S(2)}, u32[]{:S(2)}) %collective-permute-start.7) | collective-permute-done | bytes 262176 | tf_op jit(solution)/shard_map/ppermute | solution.py:216
  23.0 0.7 copy-done
  23.7 0.5 collective-permute-start.1
  24.2 3.4 %collective-permute-done.8.refs_3_ = bf16[128,1024]{1,0:T(8,128)(2,1)} collective-permute-done((bf16[128,1024]{1,0:T(8,128)(2,1)}, bf16[128,1024]{1,0:T(8,128)(2,1)}, u32[]{:S(2)}, u32[]{:S(2)}) %collective-permute-start.8) | collective-permute-done | bytes 262176 | tf_op jit(solution)/shard_map/ppermute | solution.py:216
  27.6 0.9 %copy-done.1 = bf16[128,1024]{1,0:T(8,128)(2,1)S(1)} copy-done((bf16[128,1024]{1,0:T(8,128)(2,1)S(1)}, bf16[128,1024]{1,0:T(8,128)(2,1)}, u32[]{:S(2)}) %copy-start.1) | copy-done | bytes 262168
  28.6 10.5 %local.2 = (f32[2048,1024]{1,0:T(8,128)}, bf16[8,4,2,16,128]{4,3,2,1,0:T(8,128)(2,1)}) custom-call(bf16[128,1024]{1,0:T(8,128)(2,1)S(1)} %get-tuple-element.14.refs_0_, bf16[128,1024]{1,0:T(8,128)(2,1)S(1)} %collective-permute-done.6.refs_1_, bf16[128,1024]{1,0:T(8,128)(2,1)S(1)} %copy-done.1, bf16[128,1024]{1,0:T(8,128)(2,1)} %collective-permute-done.8.refs_3_, ...), custom_call_target="tpu_custom_call" | custom-call | flops 3221225472 | bytes 8388608 | tf_op jit(solution)/shard_map/local/pallas_call | solution.py:232
  39.1 6.1 %all-to-all-start.2 = ((bf16[8,4,2,16,128]{4,3,2,1,0:T(8,128)(2,1)}), bf16[8,4,2,16,128]{4,3,2,1,0:T(8,128)(2,1)S(1)}, u32[]{:S(2)}, u32[]{:S(2)}) async-start(bf16[8,4,2,16,128]{4,3,2,1,0:T(8,128)(2,1)} %get-tuple-element.21), calls=%async_computation.2 | async-start | bytes 524288 | tf_op jit(solution)/shard_map/all_to_all | solution.py:359
  45.2 10.6 %local.3 = (f32[2048,1024]{1,0:T(8,128)}, bf16[8,4,2,16,128]{4,3,2,1,0:T(8,128)(2,1)}) custom-call(bf16[128,1024]{1,0:T(8,128)(2,1)S(1)} %get-tuple-element.24.refs_0_, bf16[128,1024]{1,0:T(8,128)(2,1)S(1)} %collective-permute-done.refs_1_, bf16[128,1024]{1,0:T(8,128)(2,1)S(1)} %collective-permute-done.1.refs_2_, ...), custom_call_target="tpu_custom_call", output_to_operand_aliasing={{0}: (11, {})} | custom-call | flops 3221225472 | bytes 8388608 | tf_op jit(solution)/shard_map/local/pallas_call | solution.py:232
  55.8 6.0 %all-to-all-start = ((bf16[8,4,2,16,128]{4,3,2,1,0:T(8,128)(2,1)}), bf16[8,4,2,16,128]{4,3,2,1,0:T(8,128)(2,1)S(1)}, u32[]{:S(2)}, u32[]{:S(2)}) async-start(bf16[8,4,2,16,128]{4,3,2,1,0:T(8,128)(2,1)} %get-tuple-element.20), calls=%async_computation | async-start | bytes 524288 | tf_op jit(solution)/shard_map/all_to_all | solution.py:359
  61.8 7.3 %shared.2.refs_3_ = f32[2048,1024]{1,0:T(8,128)} custom-call(bf16[8,4,2,16,128]{4,3,2,1,0:T(8,128)(2,1)S(1)} %all-to-all-done.2.refs_0_, s16[8,8,16,128]{3,2,1,0:T(8,128)(2,1)S(1)} %all-to-all-done.1.refs_1_, bf16[1088,256]{1,0:T(8,128)(2,1)S(1)} %broadcast_select_fusion.refs_10_.refs_2_), custom_call_target="tpu_custom_call" | custom-call | flops 3221225472 | bytes 4194304 | tf_op jit(solution)/shard_map/shared/pallas_call | solution.py:267
  69.2 2.1 %all-to-all-done.refs_0_ = bf16[8,4,2,16,128]{4,3,2,1,0:T(8,128)(2,1)S(1)} async-done(((bf16[8,4,2,16,128]{4,3,2,1,0:T(8,128)(2,1)}), bf16[8,4,2,16,128]{4,3,2,1,0:T(8,128)(2,1)S(1)}, u32[]{:S(2)}, u32[]{:S(2)}) %all-to-all-start) | async-done | bytes 262176 | tf_op jit(solution)/shard_map/all_to_all | solution.py:359
  71.3 7.3 %shared.3 = f32[2048,1024]{1,0:T(8,128)} custom-call(bf16[8,4,2,16,128]{4,3,2,1,0:T(8,128)(2,1)S(1)} %all-to-all-done.refs_0_, s16[8,8,16,128]{3,2,1,0:T(8,128)(2,1)S(1)} %all-to-all-done.1.refs_1_, bf16[1088,256]{1,0:T(8,128)(2,1)S(1)} %broadcast_select_fusion.refs_10_.refs_2_, f32[2048,1024]{1,0:T(8,128)} %shared.2.refs_3_), custom_call_target="tpu_custom_call", output_to_operand_aliasing={{}: (3, {})} | custom-call | flops 3221225472 | bytes 4194304 | tf_op jit(solution)/shard_map/shared/pallas_call | solution.py:267
  (16 shorter events, 0.8 us)
Async XLA Ops:
  0.6 19.4 %collective-permute-start.3 = (bf16[128,1024]{1,0:T(8,128)(2,1)}, bf16[128,1024]{1,0:T(8,128)(2,1)S(1)}, u32[]{:S(2)}, u32[]{:S(2)}) collective-permute-start(bf16[128,1024]{1,0:T(8,128)(2,1)} %bitcast.23), channel_id=1, source_target_pairs={{0,1},{1,0},{2,3},{3,2},{4,5},{5,4},{6,7},{7,6},{8,9},{9,8},{10,11... | collective-permute-start | bytes 786440 | tf_op jit(solution)/shard_map/ppermute | solution.py:216
  1.2 15.3 %collective-permute-start.4 = (bf16[128,1024]{1,0:T(8,128)(2,1)}, bf16[128,1024]{1,0:T(8,128)(2,1)S(1)}, u32[]{:S(2)}, u32[]{:S(2)}) collective-permute-start(bf16[128,1024]{1,0:T(8,128)(2,1)} %bitcast.24), channel_id=1, source_target_pairs={{0,2},{1,3},{2,0},{3,1},{4,6},{5,7},{6,4},{7,5},{8,10},{9,11},{10,... | collective-permute-start | bytes 786440 | tf_op jit(solution)/shard_map/ppermute | solution.py:216
  7.7 31.4 %all-to-all-start.1 = ((s16[8,8,16,128]{3,2,1,0:T(8,128)(2,1)}), s16[8,8,16,128]{3,2,1,0:T(8,128)(2,1)S(1)}, u32[]{:S(2)}, u32[]{:S(2)}) async-start(s16[8,8,16,128]{3,2,1,0:T(8,128)(2,1)} %broadcast_in_dim.20), calls=%async_computation.1 | async-start | bytes 524288 | tf_op jit(solution)/shard_map/all_to_all | solution.py:347
  13.5 6.8 %collective-permute-start.6 = (bf16[128,1024]{1,0:T(8,128)(2,1)S(1)}, bf16[128,1024]{1,0:T(8,128)(2,1)S(1)}, u32[]{:S(2)}, u32[]{:S(2)}) collective-permute-start(bf16[128,1024]{1,0:T(8,128)(2,1)S(1)} %get-tuple-element.15), channel_id=1, source_target_pairs={{0,1},{1,0},{2,3},{3,2},{4,5},{5,4},{6,7},{7,6},{8,9},{9,8},{10,11... | collective-permute-start | bytes 786440 | tf_op jit(solution)/shard_map/ppermute | solution.py:216
  13.5 9.5 %collective-permute-start.7 = (bf16[128,1024]{1,0:T(8,128)(2,1)}, bf16[128,1024]{1,0:T(8,128)(2,1)S(1)}, u32[]{:S(2)}, u32[]{:S(2)}) collective-permute-start(bf16[128,1024]{1,0:T(8,128)(2,1)} %get-tuple-element.16), channel_id=1, source_target_pairs={{0,2},{1,3},{2,0},{3,1},{4,6},{5,7},{6,4},{7,5},{8,10},{9,11},{10,... | collective-permute-start | bytes 786440 | tf_op jit(solution)/shard_map/ppermute | solution.py:216
  14.1 13.5 %collective-permute-start.8 = (bf16[128,1024]{1,0:T(8,128)(2,1)}, bf16[128,1024]{1,0:T(8,128)(2,1)}, u32[]{:S(2)}, u32[]{:S(2)}) collective-permute-start(bf16[128,1024]{1,0:T(8,128)(2,1)} %get-tuple-element.17), channel_id=1, source_target_pairs={{0,3},{1,2},{2,1},{3,0},{4,7},{5,6},{6,5},{7,4},{8,11},{9,10},{10,... | collective-permute-start | bytes 786440 | tf_op jit(solution)/shard_map/ppermute | solution.py:216
  16.5 11.2 %collective-permute-start.5 = (bf16[128,1024]{1,0:T(8,128)(2,1)S(1)}, bf16[128,1024]{1,0:T(8,128)(2,1)S(1)}, u32[]{:S(2)}, u32[]{:S(2)}) collective-permute-start(bf16[128,1024]{1,0:T(8,128)(2,1)S(1)} %collective-permute-done.4.refs_6_), channel_id=1, source_target_pairs={{0,1},{1,0},{2,3},{3,2},{4,5},{5,4},{6,7},{7,6},{8,9},{9,8},{10,11... | collective-permute-start | bytes 786440 | tf_op jit(solution)/shard_map/ppermute | solution.py:216
  20.0 25.2 %collective-permute-start.2 = (bf16[128,1024]{1,0:T(8,128)(2,1)}, bf16[128,1024]{1,0:T(8,128)(2,1)S(1)}, u32[]{:S(2)}, u32[]{:S(2)}) collective-permute-start(bf16[128,1024]{1,0:T(8,128)(2,1)} %get-tuple-element.22), channel_id=1, source_target_pairs={{0,3},{1,2},{2,1},{3,0},{4,7},{5,6},{6,5},{7,4},{8,11},{9,10},{10,... | collective-permute-start | bytes 786440 | tf_op jit(solution)/shard_map/ppermute | solution.py:216
  20.3 24.9 %collective-permute-start = (bf16[128,1024]{1,0:T(8,128)(2,1)}, bf16[128,1024]{1,0:T(8,128)(2,1)S(1)}, u32[]{:S(2)}, u32[]{:S(2)}) collective-permute-start(bf16[128,1024]{1,0:T(8,128)(2,1)} %get-tuple-element.23), channel_id=1, source_target_pairs={{0,1},{1,0},{2,3},{3,2},{4,5},{5,4},{6,7},{7,6},{8,9},{9,8},{10,11... | collective-permute-start | bytes 786440 | tf_op jit(solution)/shard_map/ppermute | solution.py:216
  23.0 0.7 copy-start
  23.7 21.5 %collective-permute-start.1 = (bf16[128,1024]{1,0:T(8,128)(2,1)}, bf16[128,1024]{1,0:T(8,128)(2,1)S(1)}, u32[]{:S(2)}, u32[]{:S(2)}) collective-permute-start(bf16[128,1024]{1,0:T(8,128)(2,1)} %get-tuple-element.25), channel_id=1, source_target_pairs={{0,2},{1,3},{2,0},{3,1},{4,6},{5,7},{6,4},{7,5},{8,10},{9,11},{10,... | collective-permute-start | bytes 786440 | tf_op jit(solution)/shard_map/ppermute | solution.py:216
  27.6 1.0 %copy-start.1 = (bf16[128,1024]{1,0:T(8,128)(2,1)S(1)}, bf16[128,1024]{1,0:T(8,128)(2,1)}, u32[]{:S(2)}) copy-start(bf16[128,1024]{1,0:T(8,128)(2,1)} %copy-done) | copy-start | bytes 786436
  39.1 16.7 %all-to-all-start.2 = ((bf16[8,4,2,16,128]{4,3,2,1,0:T(8,128)(2,1)}), bf16[8,4,2,16,128]{4,3,2,1,0:T(8,128)(2,1)S(1)}, u32[]{:S(2)}, u32[]{:S(2)}) async-start(bf16[8,4,2,16,128]{4,3,2,1,0:T(8,128)(2,1)} %get-tuple-element.21), calls=%async_computation.2 | async-start | bytes 524288 | tf_op jit(solution)/shard_map/all_to_all | solution.py:359
  55.8 15.5 %all-to-all-start = ((bf16[8,4,2,16,128]{4,3,2,1,0:T(8,128)(2,1)}), bf16[8,4,2,16,128]{4,3,2,1,0:T(8,128)(2,1)S(1)}, u32[]{:S(2)}, u32[]{:S(2)}) async-start(bf16[8,4,2,16,128]{4,3,2,1,0:T(8,128)(2,1)} %get-tuple-element.20), calls=%async_computation | async-start | bytes 524288 | tf_op jit(solution)/shard_map/all_to_all | solution.py:359

commit v3 on v2

--- a/solution.py
+++ b/solution.py
@@ -99,9 +99,12 @@
         preferred_element_type=jnp.float32,
     )
     next_ref[...] = momentum_decay * moment_ref[...] + gradient
-    for c in range(cols // WIDE):
-        span = slice(c * WIDE, c * WIDE + WIDE)
-        half_ref[:, span] = right_product(next_ref[:, span], matrix_ref[FORWARD, :])
+    for c in range(0, cols // WIDE, 2):
+        spans = [slice(b * WIDE, b * WIDE + WIDE) for b in (c, c + 1)]
+        both = jnp.concatenate([next_ref[:, span] for span in spans], axis=0)
+        both = right_product(both, matrix_ref[FORWARD, :])
+        half_ref[:, spans[0]] = both[:rows]
+        half_ref[:, spans[1]] = both[rows:]
     for p in range(rows // GROUP):
         for c in range(cols // WIDE):
             at = p * (cols // WIDE) + c

time: 79.3 us -> 79.1 us (level)
  no operation moved by 1% of the time
where the time goes in v3:
time: 79.1 us; the launch traced here: 78.4 us
  Pallas kernels  35.5 us (45%)
  starting transfers between devices  24.4 us (31%)
  waiting for transfers between devices  7.94 us (10%)
  local copies, waits for them, and re-layouts  7.67 us (10%)
  other arithmetic  2.07 us (3%)
    pallas_call x2, Pallas kernels, local_call(): pl.pallas_call(functools.partial(local_kernel, sources, kept), grid=(bloc...  20.9 us
    pallas_call x2, Pallas kernels, shared_call(): pl.pallas_call(functools.partial(shared_kernel, kept), grid=(blocks,), in...  14.6 us
    all_to_all x2, starting transfers between devices, per_device(): lax.all_to_all(message, 'rep', split_axis=0, concat_axis=0, tiled=True)  12.1 us
    ppermute x9, starting transfers between devices, swap(): return lax.ppermute(x, axis, [(i, i ^ offset) for i in range(count)])  6.54 us
    all_to_all x1, starting transfers between devices, per_device(): lax.all_to_all(copies, 'rep', split_axis=0, concat_axis=0, tiled=True)  5.81 us
    ppermute x9, waiting for transfers between devices, swap(): return lax.ppermute(x, axis, [(i, i ^ offset) for i in range(count)])  5.8 us
    dynamic_slice x2, local copies, waits for them, and re-layouts, pieces_of(): lax.dynamic_slice_in_dim(tokens, (me ^ offset) * row_count + starts[k] *...  4.19 us
    all_to_all x2, waiting for transfers between devices, per_device(): lax.all_to_all(message, 'rep', split_axis=0, concat_axis=0, tiled=True)  2.14 us
  transfers between devices with their start and end apart: 12, of which 3 were waited for; matrix products, arithmetic and copies ran while one was open for 10% of the time, Pallas kernels for 36%

profile of v3, /device:TPU:0, one launch (start us, length us, event | category | flops | bytes accessed | tf_op | source)
XLA Modules:
  0.0 78.4 jit_solution(5502236814587432897)
XLA Ops:
  0.6 0.6 collective-permute-start.3
  1.2 2.6 %collective-permute-start.4 = (bf16[128,1024]{1,0:T(8,128)(2,1)}, bf16[128,1024]{1,0:T(8,128)(2,1)S(1)}, u32[]{:S(2)}, u32[]{:S(2)}) collective-permute-start(bf16[128,1024]{1,0:T(8,128)(2,1)} %bitcast.24), channel_id=1, source_target_pairs={{0,2},{1,3},{2,0},{3,1},{4,6},{5,7},{6,4},{7,5},{8,10},{9,11},{10,... | collective-permute-start | bytes 786440 | tf_op jit(solution)/shard_map/ppermute | solution.py:219
  3.8 2.1 %dynamic-slice_bitcast_fusion.4 = (bf16[128,1024]{1,0:T(8,128)(2,1)}, bf16[128,1024]{1,0:T(8,128)(2,1)}, bf16[128,1024]{1,0:T(8,128)(2,1)S(1)}, bf16[128,1024]{1,0:T(8,128)(2,1)S(1)}) fusion(bf16[1,128,8192]{2,1,0:T(8,128)(2,1)} %param.5, s32[]{:T(128)S(6)} %select_n.43, s32[]{:T(128)S(6)} %select_n.42, s32[]{:T(128)S(6)} %select_n.41, s32[]{:T(128)S(6)} %select_n.40), kind=kLoop, calls=%fused_computation.5 | loop fusion | bytes 2097168 | tf_op jit(solution)/shard_map/dynamic_slice | solution.py:315
  5.9 1.0 %copy.10 = s32[1,512,32]{2,1,0:T(8,128)S(1)} copy(s32[1,512,32]{1,2,0:T(8,128)} %param.8) | data formatting | bytes 131072 | tf_op jit(solution)/shard_map/optimization_barrier | solution.py:334
  7.0 0.7 broadcast_in_dim.20
  7.7 5.8 %all-to-all-start.1 = ((s16[8,8,16,128]{3,2,1,0:T(8,128)(2,1)}), s16[8,8,16,128]{3,2,1,0:T(8,128)(2,1)S(1)}, u32[]{:S(2)}, u32[]{:S(2)}) async-start(s16[8,8,16,128]{3,2,1,0:T(8,128)(2,1)} %broadcast_in_dim.20), calls=%async_computation.1 | async-start | bytes 524288 | tf_op jit(solution)/shard_map/all_to_all | solution.py:350
  13.5 0.6 collective-permute-start.7
  14.1 1.3 %collective-permute-start.8 = (bf16[128,1024]{1,0:T(8,128)(2,1)}, bf16[128,1024]{1,0:T(8,128)(2,1)}, u32[]{:S(2)}, u32[]{:S(2)}) collective-permute-start(bf16[128,1024]{1,0:T(8,128)(2,1)} %get-tuple-element.17), channel_id=1, source_target_pairs={{0,3},{1,2},{2,1},{3,0},{4,7},{5,6},{6,5},{7,4},{8,11},{9,10},{10,... | collective-permute-start | bytes 786440 | tf_op jit(solution)/shard_map/ppermute | solution.py:219
  15.4 1.1 %broadcast_select_fusion.refs_10_.refs_2_ = bf16[1088,256]{1,0:T(8,128)(2,1)S(1)} fusion(bf16[1088,256]{1,0:T(8,128)(2,1)} %constant.35.clone, pred[]{:T(512)S(6)} %ge.4), kind=kLoop, calls=%fused_computation | loop fusion | flops 278528 | bytes 1114113 | tf_op jit(solution)/shard_map/jit(_where)/select_n | solution.py:342
  16.5 0.4 collective-permute-start.5
  16.9 1.0 %broadcast_select_fusion.1.refs_4_ = bf16[128,1024]{1,0:T(8,128)(2,1)S(1)} fusion(pred[]{:T(512)S(6)} %ge.4, bf16[1,128,1024]{2,1,0:T(8,128)(2,1)} %param.6), kind=kLoop, calls=%fused_computation.9 | loop fusion | flops 131072 | bytes 524289 | tf_op jit(solution)/shard_map/jit(_where)/select_n | solution.py:342
  17.9 2.1 %dynamic-slice_bitcast_fusion = (bf16[128,1024]{1,0:T(8,128)(2,1)}, bf16[128,1024]{1,0:T(8,128)(2,1)}, bf16[128,1024]{1,0:T(8,128)(2,1)S(1)}, bf16[128,1024]{1,0:T(8,128)(2,1)}) fusion(bf16[1,128,8192]{2,1,0:T(8,128)(2,1)} %param.5, s32[]{:T(128)S(6)} %select_n.47, s32[]{:T(128)S(6)} %select_n.45, s32[]{:T(128)S(6)} %select_n.44, s32[]{:T(128)S(6)} %select_n.46), kind=kLoop, calls=%fused_computation.1 | loop fusion | bytes 2097168 | tf_op jit(solution)/shard_map/dynamic_slice | solution.py:315
  20.6 2.4 %collective-permute-done.7.refs_2_ = bf16[128,1024]{1,0:T(8,128)(2,1)S(1)} collective-permute-done((bf16[128,1024]{1,0:T(8,128)(2,1)}, bf16[128,1024]{1,0:T(8,128)(2,1)S(1)}, u32[]{:S(2)}, u32[]{:S(2)}) %collective-permute-start.7) | collective-permute-done | bytes 262176 | tf_op jit(solution)/shard_map/ppermute | solution.py:219
  23.0 0.7 copy-done
  23.7 0.5 collective-permute-start.1
  24.2 3.4 %collective-permute-done.8.refs_3_ = bf16[128,1024]{1,0:T(8,128)(2,1)} collective-permute-done((bf16[128,1024]{1,0:T(8,128)(2,1)}, bf16[128,1024]{1,0:T(8,128)(2,1)}, u32[]{:S(2)}, u32[]{:S(2)}) %collective-permute-start.8) | collective-permute-done | bytes 262176 | tf_op jit(solution)/shard_map/ppermute | solution.py:219
  27.6 0.9 %copy-done.1 = bf16[128,1024]{1,0:T(8,128)(2,1)S(1)} copy-done((bf16[128,1024]{1,0:T(8,128)(2,1)S(1)}, bf16[128,1024]{1,0:T(8,128)(2,1)}, u32[]{:S(2)}) %copy-start.1) | copy-done | bytes 262168
  28.6 10.4 %local.2 = (f32[2048,1024]{1,0:T(8,128)}, bf16[8,4,2,16,128]{4,3,2,1,0:T(8,128)(2,1)}) custom-call(bf16[128,1024]{1,0:T(8,128)(2,1)S(1)} %get-tuple-element.14.refs_0_, bf16[128,1024]{1,0:T(8,128)(2,1)S(1)} %collective-permute-done.6.refs_1_, bf16[128,1024]{1,0:T(8,128)(2,1)S(1)} %copy-done.1, bf16[128,1024]{1,0:T(8,128)(2,1)} %collective-permute-done.8.refs_3_, ...), custom_call_target="tpu_custom_call" | custom-call | flops 3221225472 | bytes 8388608 | tf_op jit(solution)/shard_map/local/pallas_call | solution.py:235
  39.0 6.1 %all-to-all-start.2 = ((bf16[8,4,2,16,128]{4,3,2,1,0:T(8,128)(2,1)}), bf16[8,4,2,16,128]{4,3,2,1,0:T(8,128)(2,1)S(1)}, u32[]{:S(2)}, u32[]{:S(2)}) async-start(bf16[8,4,2,16,128]{4,3,2,1,0:T(8,128)(2,1)} %get-tuple-element.21), calls=%async_computation.2 | async-start | bytes 524288 | tf_op jit(solution)/shard_map/all_to_all | solution.py:362
  45.1 10.5 %local.3 = (f32[2048,1024]{1,0:T(8,128)}, bf16[8,4,2,16,128]{4,3,2,1,0:T(8,128)(2,1)}) custom-call(bf16[128,1024]{1,0:T(8,128)(2,1)S(1)} %get-tuple-element.24.refs_0_, bf16[128,1024]{1,0:T(8,128)(2,1)S(1)} %collective-permute-done.refs_1_, bf16[128,1024]{1,0:T(8,128)(2,1)S(1)} %collective-permute-done.1.refs_2_, ...), custom_call_target="tpu_custom_call", output_to_operand_aliasing={{0}: (11, {})} | custom-call | flops 3221225472 | bytes 8388608 | tf_op jit(solution)/shard_map/local/pallas_call | solution.py:235
  55.6 6.0 %all-to-all-start = ((bf16[8,4,2,16,128]{4,3,2,1,0:T(8,128)(2,1)}), bf16[8,4,2,16,128]{4,3,2,1,0:T(8,128)(2,1)S(1)}, u32[]{:S(2)}, u32[]{:S(2)}) async-start(bf16[8,4,2,16,128]{4,3,2,1,0:T(8,128)(2,1)} %get-tuple-element.20), calls=%async_computation | async-start | bytes 524288 | tf_op jit(solution)/shard_map/all_to_all | solution.py:362
  61.6 7.3 %shared.2.refs_3_ = f32[2048,1024]{1,0:T(8,128)} custom-call(bf16[8,4,2,16,128]{4,3,2,1,0:T(8,128)(2,1)S(1)} %all-to-all-done.2.refs_0_, s16[8,8,16,128]{3,2,1,0:T(8,128)(2,1)S(1)} %all-to-all-done.1.refs_1_, bf16[1088,256]{1,0:T(8,128)(2,1)S(1)} %broadcast_select_fusion.refs_10_.refs_2_), custom_call_target="tpu_custom_call" | custom-call | flops 3221225472 | bytes 4194304 | tf_op jit(solution)/shard_map/shared/pallas_call | solution.py:270
  68.9 2.1 %all-to-all-done.refs_0_ = bf16[8,4,2,16,128]{4,3,2,1,0:T(8,128)(2,1)S(1)} async-done(((bf16[8,4,2,16,128]{4,3,2,1,0:T(8,128)(2,1)}), bf16[8,4,2,16,128]{4,3,2,1,0:T(8,128)(2,1)S(1)}, u32[]{:S(2)}, u32[]{:S(2)}) %all-to-all-start) | async-done | bytes 262176 | tf_op jit(solution)/shard_map/all_to_all | solution.py:362
  71.0 7.3 %shared.3 = f32[2048,1024]{1,0:T(8,128)} custom-call(bf16[8,4,2,16,128]{4,3,2,1,0:T(8,128)(2,1)S(1)} %all-to-all-done.refs_0_, s16[8,8,16,128]{3,2,1,0:T(8,128)(2,1)S(1)} %all-to-all-done.1.refs_1_, bf16[1088,256]{1,0:T(8,128)(2,1)S(1)} %broadcast_select_fusion.refs_10_.refs_2_, f32[2048,1024]{1,0:T(8,128)} %shared.2.refs_3_), custom_call_target="tpu_custom_call", output_to_operand_aliasing={{}: (3, {})} | custom-call | flops 3221225472 | bytes 4194304 | tf_op jit(solution)/shard_map/shared/pallas_call | solution.py:270
  (16 shorter events, 0.8 us)
Async XLA Ops:
  0.6 19.4 %collective-permute-start.3 = (bf16[128,1024]{1,0:T(8,128)(2,1)}, bf16[128,1024]{1,0:T(8,128)(2,1)S(1)}, u32[]{:S(2)}, u32[]{:S(2)}) collective-permute-start(bf16[128,1024]{1,0:T(8,128)(2,1)} %bitcast.23), channel_id=1, source_target_pairs={{0,1},{1,0},{2,3},{3,2},{4,5},{5,4},{6,7},{7,6},{8,9},{9,8},{10,11... | collective-permute-start | bytes 786440 | tf_op jit(solution)/shard_map/ppermute | solution.py:219
  1.2 15.3 %collective-permute-start.4 = (bf16[128,1024]{1,0:T(8,128)(2,1)}, bf16[128,1024]{1,0:T(8,128)(2,1)S(1)}, u32[]{:S(2)}, u32[]{:S(2)}) collective-permute-start(bf16[128,1024]{1,0:T(8,128)(2,1)} %bitcast.24), channel_id=1, source_target_pairs={{0,2},{1,3},{2,0},{3,1},{4,6},{5,7},{6,4},{7,5},{8,10},{9,11},{10,... | collective-permute-start | bytes 786440 | tf_op jit(solution)/shard_map/ppermute | solution.py:219
  7.7 31.3 %all-to-all-start.1 = ((s16[8,8,16,128]{3,2,1,0:T(8,128)(2,1)}), s16[8,8,16,128]{3,2,1,0:T(8,128)(2,1)S(1)}, u32[]{:S(2)}, u32[]{:S(2)}) async-start(s16[8,8,16,128]{3,2,1,0:T(8,128)(2,1)} %broadcast_in_dim.20), calls=%async_computation.1 | async-start | bytes 524288 | tf_op jit(solution)/shard_map/all_to_all | solution.py:350
  13.5 6.8 %collective-permute-start.6 = (bf16[128,1024]{1,0:T(8,128)(2,1)S(1)}, bf16[128,1024]{1,0:T(8,128)(2,1)S(1)}, u32[]{:S(2)}, u32[]{:S(2)}) collective-permute-start(bf16[128,1024]{1,0:T(8,128)(2,1)S(1)} %get-tuple-element.15), channel_id=1, source_target_pairs={{0,1},{1,0},{2,3},{3,2},{4,5},{5,4},{6,7},{7,6},{8,9},{9,8},{10,11... | collective-permute-start | bytes 786440 | tf_op jit(solution)/shard_map/ppermute | solution.py:219
  13.5 9.5 %collective-permute-start.7 = (bf16[128,1024]{1,0:T(8,128)(2,1)}, bf16[128,1024]{1,0:T(8,128)(2,1)S(1)}, u32[]{:S(2)}, u32[]{:S(2)}) collective-permute-start(bf16[128,1024]{1,0:T(8,128)(2,1)} %get-tuple-element.16), channel_id=1, source_target_pairs={{0,2},{1,3},{2,0},{3,1},{4,6},{5,7},{6,4},{7,5},{8,10},{9,11},{10,... | collective-permute-start | bytes 786440 | tf_op jit(solution)/shard_map/ppermute | solution.py:219
  14.1 13.5 %collective-permute-start.8 = (bf16[128,1024]{1,0:T(8,128)(2,1)}, bf16[128,1024]{1,0:T(8,128)(2,1)}, u32[]{:S(2)}, u32[]{:S(2)}) collective-permute-start(bf16[128,1024]{1,0:T(8,128)(2,1)} %get-tuple-element.17), channel_id=1, source_target_pairs={{0,3},{1,2},{2,1},{3,0},{4,7},{5,6},{6,5},{7,4},{8,11},{9,10},{10,... | collective-permute-start | bytes 786440 | tf_op jit(solution)/shard_map/ppermute | solution.py:219
  16.5 11.2 %collective-permute-start.5 = (bf16[128,1024]{1,0:T(8,128)(2,1)S(1)}, bf16[128,1024]{1,0:T(8,128)(2,1)S(1)}, u32[]{:S(2)}, u32[]{:S(2)}) collective-permute-start(bf16[128,1024]{1,0:T(8,128)(2,1)S(1)} %collective-permute-done.4.refs_6_), channel_id=1, source_target_pairs={{0,1},{1,0},{2,3},{3,2},{4,5},{5,4},{6,7},{7,6},{8,9},{9,8},{10,11... | collective-permute-start | bytes 786440 | tf_op jit(solution)/shard_map/ppermute | solution.py:219
  20.0 25.1 %collective-permute-start.2 = (bf16[128,1024]{1,0:T(8,128)(2,1)}, bf16[128,1024]{1,0:T(8,128)(2,1)S(1)}, u32[]{:S(2)}, u32[]{:S(2)}) collective-permute-start(bf16[128,1024]{1,0:T(8,128)(2,1)} %get-tuple-element.22), channel_id=1, source_target_pairs={{0,3},{1,2},{2,1},{3,0},{4,7},{5,6},{6,5},{7,4},{8,11},{9,10},{10,... | collective-permute-start | bytes 786440 | tf_op jit(solution)/shard_map/ppermute | solution.py:219
  20.3 24.8 %collective-permute-start = (bf16[128,1024]{1,0:T(8,128)(2,1)}, bf16[128,1024]{1,0:T(8,128)(2,1)S(1)}, u32[]{:S(2)}, u32[]{:S(2)}) collective-permute-start(bf16[128,1024]{1,0:T(8,128)(2,1)} %get-tuple-element.23), channel_id=1, source_target_pairs={{0,1},{1,0},{2,3},{3,2},{4,5},{5,4},{6,7},{7,6},{8,9},{9,8},{10,11... | collective-permute-start | bytes 786440 | tf_op jit(solution)/shard_map/ppermute | solution.py:219
  23.0 0.7 copy-start
  23.7 21.4 %collective-permute-start.1 = (bf16[128,1024]{1,0:T(8,128)(2,1)}, bf16[128,1024]{1,0:T(8,128)(2,1)S(1)}, u32[]{:S(2)}, u32[]{:S(2)}) collective-permute-start(bf16[128,1024]{1,0:T(8,128)(2,1)} %get-tuple-element.25), channel_id=1, source_target_pairs={{0,2},{1,3},{2,0},{3,1},{4,6},{5,7},{6,4},{7,5},{8,10},{9,11},{10,... | collective-permute-start | bytes 786440 | tf_op jit(solution)/shard_map/ppermute | solution.py:219
  27.6 1.0 %copy-start.1 = (bf16[128,1024]{1,0:T(8,128)(2,1)S(1)}, bf16[128,1024]{1,0:T(8,128)(2,1)}, u32[]{:S(2)}) copy-start(bf16[128,1024]{1,0:T(8,128)(2,1)} %copy-done) | copy-start | bytes 786436
  39.0 16.6 %all-to-all-start.2 = ((bf16[8,4,2,16,128]{4,3,2,1,0:T(8,128)(2,1)}), bf16[8,4,2,16,128]{4,3,2,1,0:T(8,128)(2,1)S(1)}, u32[]{:S(2)}, u32[]{:S(2)}) async-start(bf16[8,4,2,16,128]{4,3,2,1,0:T(8,128)(2,1)} %get-tuple-element.21), calls=%async_computation.2 | async-start | bytes 524288 | tf_op jit(solution)/shard_map/all_to_all | solution.py:362
  55.6 15.5 %all-to-all-start = ((bf16[8,4,2,16,128]{4,3,2,1,0:T(8,128)(2,1)}), bf16[8,4,2,16,128]{4,3,2,1,0:T(8,128)(2,1)S(1)}, u32[]{:S(2)}, u32[]{:S(2)}) async-start(bf16[8,4,2,16,128]{4,3,2,1,0:T(8,128)(2,1)} %get-tuple-element.20), calls=%async_computation | async-start | bytes 524288 | tf_op jit(solution)/shard_map/all_to_all | solution.py:362
